TPU v7x, 128 devices: a whole 4x4x4 slice. The times are simulated.
128 devices in a mesh: expert: 32 (over z, x, core), shard: 4 (over y).
Axes of the slice: x: 4, y: 4, z: 4, core: 2. Of those that a mesh axis runs over, the one named last changes fastest.
Arguments:
- tokens: bfloat16 [32768, 1024], P(('expert', 'shard')), may hold values from -6 to 6
- segments: int32 [32, 1024], P('expert', 'shard'), may hold values from 0 to 3, never falling along the last dimension, each value on 1 to 768 neighbouring positions
- expert_ids: int32 [32768, 8], P(('expert', 'shard')), may hold values from 0 to 31, all different within a row; in each aligned block of 256 rows (0 to 255, 256 to 511, ...) at most 72 rows name the same one
- attn_norm: bfloat16 [1024], P('shard'), may hold values from 0.5 to 1.5
- query_weight: bfloat16 [1024, 1024], P('shard'), may hold values from -0.1875 to 0.1875
- key_matrix: bfloat16 [1024, 512], P('shard'), may hold values from -0.1875 to 0.1875
- value_matrix: bfloat16 [1024, 512], P('shard'), may hold values from -0.1875 to 0.1875
- output_weight: bfloat16 [1024, 1024], P(None, 'shard'), may hold values from -1.5 to 1.5
- ffn_norm: bfloat16 [1024], P('shard'), may hold values from 0.5 to 1.5
- router_weight: bfloat16 [1024, 32], P('shard'), may hold values from -0.1875 to 0.1875
- gate_weight: bfloat16 [32, 1024, 512], P('expert', 'shard'), may hold values from -0.1875 to 0.1875
- up_weight: bfloat16 [32, 1024, 512], P('expert', 'shard'), may hold values from -0.1875 to 0.1875
- down_weight: bfloat16 [32, 512, 1024], P('expert', None, 'shard'), may hold values from -0.75 to 0.75
- cotangent: bfloat16 [32768, 1024], P(('expert', 'shard')), may hold values from -24 to 24
Outputs:
- output: bfloat16 [32768, 1024], P(('expert', 'shard'))
- d_tokens: bfloat16 [32768, 1024], P(('expert', 'shard'))
- d_attn_norm: float32 [1024], P('shard')
- d_query: float32 [1024, 1024], P('shard')
- d_key: float32 [1024, 512], P('shard')
- d_value: float32 [1024, 512], P('shard')
- d_output_weight: float32 [1024, 1024], P(None, 'shard')
- d_ffn_norm: float32 [1024], P('shard')
- d_router: float32 [1024, 32], P('shard')
- d_gate: float32 [32, 1024, 512], P('expert', 'shard')
- d_up: float32 [32, 1024, 512], P('expert', 'shard')
- d_down: float32 [32, 512, 1024], P('expert', None, 'shard')
Inputs may be any that keep to these rules, and one draw needn't show every extreme that they name: `expert_ids`: each row names 8 different experts. Among the 256 rows of one device no expert is named more than 72 times, a bound that some block reaches. `segments`: along each sequence the numbers never fall; each document has 1 to 768 tokens, and one has exactly 768.
All inputs are finite; a program needn't handle non-finite values.
Results may differ from a plain program's by a relative error of at most 0.025.
Values may be sent and summed in bfloat16 or wider, within the bound.
A program may use at most 192 MiB of HBM per device.

v0:
```python
import jax
import jax.numpy as jnp
from jax import lax
from jax.sharding import PartitionSpec as P

MODEL_WIDTH = 1024
QUERY_HEADS = 16
KEY_VALUE_HEADS = 8
HEAD_SIZE = 64
TOPK = 8


EPS = 1e-05
BASE = 10000.0


def rms_scale(values):
    return lax.rsqrt(jnp.mean(values * values, axis=-1, keepdims=True) + EPS)


def rope_tables(positions):
    half_dim = HEAD_SIZE // 2
    inverse = BASE ** (-jnp.arange(half_dim, dtype=jnp.float32) * 2.0 / HEAD_SIZE)
    angles = positions.astype(jnp.float32)[:, None] * inverse[None, :]
    return (jnp.cos(angles)[:, None, :], jnp.sin(angles)[:, None, :])


def apply_rotary(values, cosine_table, sine_table):
    half_dim = values.shape[-1] // 2
    first_half = values[..., :half_dim]
    second_half = values[..., half_dim:]
    return jnp.concatenate(
        [
            first_half * cosine_table - second_half * sine_table,
            second_half * cosine_table + first_half * sine_table,
        ],
        axis=-1,
    )


def reverse_rotary(grads, cosine_table, sine_table):
    half_dim = grads.shape[-1] // 2
    first_half = grads[..., :half_dim]
    second_half = grads[..., half_dim:]
    return jnp.concatenate(
        [
            first_half * cosine_table + second_half * sine_table,
            second_half * cosine_table - first_half * sine_table,
        ],
        axis=-1,
    )


def gather_weights(weights):
    return (
        lax.all_gather(weights[0], "shard", axis=0, tiled=True),
        lax.all_gather(weights[1], "shard", axis=0, tiled=True),
        lax.all_gather(weights[2], "shard", axis=0, tiled=True),
        lax.all_gather(weights[3], "shard", axis=0, tiled=True),
        lax.all_gather(weights[4], "shard", axis=1, tiled=True),
        lax.all_gather(weights[5], "shard", axis=0, tiled=True),
        lax.all_gather(weights[6], "shard", axis=0, tiled=True),
        lax.all_gather(weights[7], "shard", axis=1, tiled=True),
        lax.all_gather(weights[8], "shard", axis=1, tiled=True),
        lax.all_gather(weights[9], "shard", axis=2, tiled=True),
    )


def gather_weights_again(weights):
    return (
        lax.all_gather(weights[0], "shard", axis=0, tiled=True),
        lax.all_gather(weights[1], "shard", axis=0, tiled=True),
        lax.all_gather(weights[2], "shard", axis=0, tiled=True),
        lax.all_gather(weights[3], "shard", axis=0, tiled=True),
        lax.all_gather(weights[4], "shard", axis=1, tiled=True),
        lax.all_gather(weights[5], "shard", axis=0, tiled=True),
        lax.all_gather(weights[6], "shard", axis=0, tiled=True),
        lax.all_gather(weights[7], "shard", axis=1, tiled=True),
        lax.all_gather(weights[8], "shard", axis=1, tiled=True),
        lax.all_gather(weights[9], "shard", axis=2, tiled=True),
    )


def gather_keys(pieces):
    return (
        lax.all_gather(pieces[0], "shard", axis=0, tiled=True),
        lax.all_gather(pieces[1], "shard", axis=0, tiled=True),
        lax.all_gather(pieces[2], "shard", axis=0, tiled=True),
    )


def gather_keys_again(pieces):
    return (
        lax.all_gather(pieces[0], "shard", axis=0, tiled=True),
        lax.all_gather(pieces[1], "shard", axis=0, tiled=True),
        lax.all_gather(pieces[2], "shard", axis=0, tiled=True),
    )


def score_table(query_by_group, keys_gathered, seg_local, seg_all, positions):
    key_head_rows = keys_gathered.reshape(keys_gathered.shape[0], KEY_VALUE_HEADS, HEAD_SIZE)
    scores = jnp.einsum(
        "tgrd,sgd->tgrs", query_by_group, key_head_rows, preferred_element_type=jnp.float32
    ) * HEAD_SIZE ** (-0.5)
    key_positions = jnp.arange(keys_gathered.shape[0], dtype=jnp.int32)
    allowed = (seg_local[:, None] == seg_all[None, :]) & (
        key_positions[None, :] <= positions[:, None]
    )
    return (scores, allowed[:, None, None, :])


def per_device(
    tokens,
    segments,
    expert_ids,
    attn_norm,
    query_weight,
    key_matrix,
    value_matrix,
    output_weight,
    ffn_norm,
    router_weight,
    gate_weight,
    up_weight,
    down_weight,
    cotangent,
):
    single_float = jnp.float32
    brain_float_half = jnp.bfloat16
    shard_index = lax.axis_index("shard")
    shard_rows_local = tokens.shape[0]
    query_group_width = QUERY_HEADS // KEY_VALUE_HEADS
    experts = router_weight.shape[1]
    capacity = min(
        shard_rows_local,
        shard_rows_local * TOPK // experts + shard_rows_local * TOPK // (8 * experts),
    )
    local_weights = (
        attn_norm,
        query_weight,
        key_matrix,
        value_matrix,
        output_weight,
        ffn_norm,
        router_weight,
        gate_weight,
        up_weight,
        down_weight,
    )
    full = gather_weights(local_weights)
    (
        norm_one,
        w_query,
        key_projection_weight,
        w_value,
        w_output,
        norm_two,
        w_router,
        w_gate,
        w_up,
        w_down,
    ) = full
    gain_one = norm_one.astype(single_float)
    gain_two = norm_two.astype(single_float)
    x_float = tokens.astype(single_float)
    scale_one = rms_scale(x_float)
    normed_one = x_float * scale_one
    hidden_first = (normed_one * gain_one).astype(brain_float_half)
    positions = shard_index * shard_rows_local + jnp.arange(shard_rows_local, dtype=jnp.int32)
    cosine_table, sine_table = rope_tables(positions)
    query_rotated = apply_rotary(
        jnp.dot(hidden_first, w_query, preferred_element_type=single_float).reshape(
            shard_rows_local, QUERY_HEADS, HEAD_SIZE
        ),
        cosine_table,
        sine_table,
    ).astype(brain_float_half)
    key_rotated = (
        apply_rotary(
            jnp.dot(
                hidden_first, key_projection_weight, preferred_element_type=single_float
            ).reshape(shard_rows_local, KEY_VALUE_HEADS, HEAD_SIZE),
            cosine_table,
            sine_table,
        )
        .astype(brain_float_half)
        .reshape(shard_rows_local, KEY_VALUE_HEADS * HEAD_SIZE)
    )
    value_row_block = jnp.dot(hidden_first, w_value, preferred_element_type=single_float).astype(
        brain_float_half
    )
    seg_local = segments.reshape(shard_rows_local).astype(brain_float_half)
    keys_gathered, values_gathered, seg_all = gather_keys((key_rotated, value_row_block, seg_local))
    query_by_group = query_rotated.reshape(
        shard_rows_local, KEY_VALUE_HEADS, query_group_width, HEAD_SIZE
    )
    scores, allowed = score_table(query_by_group, keys_gathered, seg_local, seg_all, positions)
    exponent = jnp.where(allowed, jnp.exp(scores), 0.0)
    log_total = jnp.log(jnp.sum(exponent, axis=-1))
    attention_probs = jnp.where(allowed, jnp.exp(scores - log_total[..., None]), 0.0).astype(
        brain_float_half
    )
    value_head_rows = values_gathered.reshape(values_gathered.shape[0], KEY_VALUE_HEADS, HEAD_SIZE)
    attended4 = jnp.einsum(
        "qaim,mal->qail", attention_probs, value_head_rows, preferred_element_type=single_float
    ).astype(brain_float_half)
    attended_rows = attended4.reshape(shard_rows_local, QUERY_HEADS * HEAD_SIZE)
    resid = x_float + jnp.dot(attended_rows, w_output, preferred_element_type=single_float)
    scale_two = rms_scale(resid)
    normed_two = resid * scale_two
    hidden_two = (normed_two * gain_two).astype(brain_float_half)
    logits = jnp.dot(hidden_two, w_router, preferred_element_type=single_float)
    onehot = expert_ids[:, :, None] == jnp.arange(experts, dtype=jnp.int32)[None, None, :]
    onehot_float = onehot.astype(single_float)
    chosen = jnp.sum(onehot_float * logits[:, None, :], axis=-1)
    gate_exp = jnp.exp(chosen)
    gates = gate_exp / jnp.sum(gate_exp, axis=-1, keepdims=True)
    flat_ids = expert_ids.reshape(-1)
    onehot_int = onehot.reshape(shard_rows_local * TOPK, experts).astype(jnp.int32)
    before = jnp.cumsum(onehot_int, axis=0) - onehot_int
    slot_pos = jnp.sum(before * onehot_int, axis=-1)
    source_row = jnp.arange(shard_rows_local * TOPK, dtype=jnp.int32) // TOPK
    send_rows = (
        jnp.zeros((experts, capacity, MODEL_WIDTH), brain_float_half)
        .at[flat_ids, slot_pos]
        .set(hidden_two[source_row])
    )
    received = lax.all_to_all(send_rows, "expert", split_axis=0, concat_axis=0, tiled=True)
    flat_in = received.reshape(-1, MODEL_WIDTH)
    gate_mat = w_gate[0]
    up_mat = w_up[0]
    down_mat = w_down[0]
    gate_pre = jnp.dot(flat_in, gate_mat, preferred_element_type=single_float)
    up_pre = jnp.dot(flat_in, up_mat, preferred_element_type=single_float)
    sigmoid_pre = jax.nn.sigmoid(gate_pre)
    activ = gate_pre * sigmoid_pre
    mid = (activ * up_pre).astype(brain_float_half)
    result = (
        jnp.dot(mid, down_mat, preferred_element_type=single_float)
        .astype(brain_float_half)
        .reshape(experts, capacity, MODEL_WIDTH)
    )
    returned = lax.all_to_all(result, "expert", split_axis=0, concat_axis=0, tiled=True)
    slot_out = (
        returned[flat_ids, slot_pos]
        .astype(single_float)
        .reshape(shard_rows_local, TOPK, MODEL_WIDTH)
    )
    combined = jnp.sum(gates[:, :, None] * slot_out, axis=1)
    output = (resid + combined).astype(brain_float_half)
    cot_float = cotangent.astype(single_float)
    d_gates = jnp.sum(cot_float[:, None, :] * slot_out, axis=-1)
    d_slot = (
        (gates[:, :, None] * cot_float[:, None, :])
        .astype(brain_float_half)
        .reshape(shard_rows_local * TOPK, MODEL_WIDTH)
    )
    send_grads = (
        jnp.zeros((experts, capacity, MODEL_WIDTH), brain_float_half)
        .at[flat_ids, slot_pos]
        .set(d_slot)
    )
    recv_grads = lax.all_to_all(
        send_grads, "expert", split_axis=0, concat_axis=0, tiled=True
    ).reshape(-1, MODEL_WIDTH)
    d_mid = jnp.einsum("nd,fd->nf", recv_grads, down_mat, preferred_element_type=single_float)
    grad_down = jnp.einsum("nf,nd->fd", mid, recv_grads, preferred_element_type=single_float)
    d_gate_pre = (d_mid * up_pre * sigmoid_pre * (1.0 + gate_pre * (1.0 - sigmoid_pre))).astype(
        brain_float_half
    )
    d_up_pre = (d_mid * activ).astype(brain_float_half)
    grad_gate = jnp.einsum("nd,nf->df", flat_in, d_gate_pre, preferred_element_type=single_float)
    grad_up = jnp.einsum("nd,nf->df", flat_in, d_up_pre, preferred_element_type=single_float)
    d_rows = (
        (
            jnp.einsum("nf,df->nd", d_gate_pre, gate_mat, preferred_element_type=single_float)
            + jnp.einsum("nf,df->nd", d_up_pre, up_mat, preferred_element_type=single_float)
        )
        .astype(brain_float_half)
        .reshape(experts, capacity, MODEL_WIDTH)
    )
    back_grads = lax.all_to_all(d_rows, "expert", split_axis=0, concat_axis=0, tiled=True)
    d_hidden_moe = jnp.sum(
        back_grads[flat_ids, slot_pos]
        .astype(single_float)
        .reshape(shard_rows_local, TOPK, MODEL_WIDTH),
        axis=1,
    )
    d_gate, d_up, d_down = (
        lax.psum_scatter(
            grad_gate[None].astype(jnp.bfloat16), "shard", scatter_dimension=1, tiled=True
        ).astype(jnp.float32),
        lax.psum_scatter(
            grad_up[None].astype(jnp.bfloat16), "shard", scatter_dimension=1, tiled=True
        ).astype(jnp.float32),
        lax.psum_scatter(
            grad_down[None].astype(jnp.bfloat16), "shard", scatter_dimension=2, tiled=True
        ).astype(jnp.float32),
    )
    full_back = gather_weights_again(local_weights)
    keys_backward, values_backward, seg_back = gather_keys_again(
        (key_rotated, value_row_block, seg_local)
    )
    (
        norm_one_b,
        query_back,
        key_back,
        value_back,
        output_back,
        norm_two_b,
        router_back,
        gate_unused,
        up_unused,
        down_unused,
    ) = full_back
    d_chosen = gates * (d_gates - jnp.sum(gates * d_gates, axis=-1, keepdims=True))
    d_logits = jnp.sum(onehot_float * d_chosen[:, :, None], axis=1).astype(brain_float_half)
    grad_router = jnp.einsum("td,te->de", hidden_two, d_logits, preferred_element_type=single_float)
    d_hidden_two = d_hidden_moe + jnp.einsum(
        "te,de->td", d_logits, router_back, preferred_element_type=single_float
    )
    grad_norm_two = jnp.sum(d_hidden_two * normed_two, axis=0)
    m_two = d_hidden_two * norm_two_b.astype(single_float)
    d_resid = cot_float + scale_two * (
        m_two - normed_two * jnp.mean(m_two * normed_two, axis=-1, keepdims=True)
    )
    d_attn = d_resid.astype(brain_float_half)
    grad_output = jnp.einsum(
        "tc,td->cd", attended_rows, d_attn, preferred_element_type=single_float
    )
    grad_attended = jnp.einsum(
        "td,cd->tc", d_attn, output_back, preferred_element_type=single_float
    ).astype(brain_float_half)
    scores_back, allowed_back = score_table(
        query_by_group, keys_backward, seg_local, seg_back, positions
    )
    probs_full = jnp.where(allowed_back, jnp.exp(scores_back - log_total[..., None]), 0.0)
    probs_round = probs_full.astype(brain_float_half)
    grad_attended_four = grad_attended.reshape(
        shard_rows_local, KEY_VALUE_HEADS, query_group_width, HEAD_SIZE
    )
    value_head_rows_backward = values_backward.reshape(
        values_backward.shape[0], KEY_VALUE_HEADS, HEAD_SIZE
    )
    grad_values = jnp.einsum(
        "qkaz,qkay->zky", probs_round, grad_attended_four, preferred_element_type=single_float
    )
    d_probs = jnp.einsum(
        "tgrd,sgd->tgrs",
        grad_attended_four,
        value_head_rows_backward,
        preferred_element_type=single_float,
    )
    softmax_correction = jnp.sum(
        grad_attended_four.astype(single_float) * attended4.astype(single_float), axis=-1
    )
    grad_scores = (
        probs_full * (d_probs - softmax_correction[..., None]) * HEAD_SIZE ** (-0.5)
    ).astype(brain_float_half)
    key_head_rows_backward = keys_backward.reshape(
        keys_backward.shape[0], KEY_VALUE_HEADS, HEAD_SIZE
    )
    grad_query_unrotated = jnp.einsum(
        "qaim,mal->qail", grad_scores, key_head_rows_backward, preferred_element_type=single_float
    )
    grad_key_unrotated = jnp.einsum(
        "qkaz,qkay->zky", grad_scores, query_by_group, preferred_element_type=single_float
    )
    key_total_count = keys_backward.shape[0]
    local_key_gradient, own_dv = (
        lax.psum_scatter(
            grad_key_unrotated.reshape(key_total_count, KEY_VALUE_HEADS * HEAD_SIZE).astype(
                jnp.bfloat16
            ),
            "shard",
            scatter_dimension=0,
            tiled=True,
        ).astype(jnp.float32),
        lax.psum_scatter(
            grad_values.reshape(key_total_count, KEY_VALUE_HEADS * HEAD_SIZE).astype(jnp.bfloat16),
            "shard",
            scatter_dimension=0,
            tiled=True,
        ).astype(jnp.float32),
    )
    dq_rows = (
        reverse_rotary(
            grad_query_unrotated.reshape(shard_rows_local, QUERY_HEADS, HEAD_SIZE),
            cosine_table,
            sine_table,
        )
        .astype(brain_float_half)
        .reshape(shard_rows_local, QUERY_HEADS * HEAD_SIZE)
    )
    grad_key_rows = (
        reverse_rotary(
            local_key_gradient.reshape(shard_rows_local, KEY_VALUE_HEADS, HEAD_SIZE),
            cosine_table,
            sine_table,
        )
        .astype(brain_float_half)
        .reshape(shard_rows_local, KEY_VALUE_HEADS * HEAD_SIZE)
    )
    grad_value_rows = own_dv.astype(brain_float_half)
    grad_query = jnp.einsum("td,tc->dc", hidden_first, dq_rows, preferred_element_type=single_float)
    grad_key = jnp.einsum(
        "td,tc->dc", hidden_first, grad_key_rows, preferred_element_type=single_float
    )
    grad_value = jnp.einsum(
        "td,tc->dc", hidden_first, grad_value_rows, preferred_element_type=single_float
    )
    d_hidden_one = (
        jnp.einsum("tc,dc->td", dq_rows, query_back, preferred_element_type=single_float)
        + jnp.einsum("tc,dc->td", grad_key_rows, key_back, preferred_element_type=single_float)
        + jnp.einsum("tc,dc->td", grad_value_rows, value_back, preferred_element_type=single_float)
    )
    grad_norm_one = jnp.sum(d_hidden_one * normed_one, axis=0)
    m_one = d_hidden_one * norm_one_b.astype(single_float)
    d_tokens = (
        d_resid
        + scale_one * (m_one - normed_one * jnp.mean(m_one * normed_one, axis=-1, keepdims=True))
    ).astype(brain_float_half)
    dense_terms = (
        grad_norm_one,
        grad_query,
        grad_key,
        grad_value,
        grad_output,
        grad_norm_two,
        grad_router,
    )
    partial_sums = (
        lax.psum_scatter(
            dense_terms[0].astype(jnp.bfloat16), "shard", scatter_dimension=0, tiled=True
        ).astype(jnp.float32),
        lax.psum_scatter(
            dense_terms[1].astype(jnp.bfloat16), "shard", scatter_dimension=0, tiled=True
        ).astype(jnp.float32),
        lax.psum_scatter(
            dense_terms[2].astype(jnp.bfloat16), "shard", scatter_dimension=0, tiled=True
        ).astype(jnp.float32),
        lax.psum_scatter(
            dense_terms[3].astype(jnp.bfloat16), "shard", scatter_dimension=0, tiled=True
        ).astype(jnp.float32),
        lax.psum_scatter(
            dense_terms[4].astype(jnp.bfloat16), "shard", scatter_dimension=1, tiled=True
        ).astype(jnp.float32),
        lax.psum_scatter(
            dense_terms[5].astype(jnp.bfloat16), "shard", scatter_dimension=0, tiled=True
        ).astype(jnp.float32),
        lax.psum_scatter(
            dense_terms[6].astype(jnp.bfloat16), "shard", scatter_dimension=0, tiled=True
        ).astype(jnp.float32),
    )
    dense_out = (
        lax.psum(partial_sums[0].astype(jnp.bfloat16), "expert").astype(jnp.float32),
        lax.psum(partial_sums[1].astype(jnp.bfloat16), "expert").astype(jnp.float32),
        lax.psum(partial_sums[2].astype(jnp.bfloat16), "expert").astype(jnp.float32),
        lax.psum(partial_sums[3].astype(jnp.bfloat16), "expert").astype(jnp.float32),
        lax.psum(partial_sums[4].astype(jnp.bfloat16), "expert").astype(jnp.float32),
        lax.psum(partial_sums[5].astype(jnp.bfloat16), "expert").astype(jnp.float32),
        lax.psum(partial_sums[6].astype(jnp.bfloat16), "expert").astype(jnp.float32),
    )
    d_attn_norm, d_query, d_key, d_value, d_output_weight, d_ffn_norm, d_router = dense_out
    return (
        output,
        d_tokens,
        d_attn_norm,
        d_query,
        d_key,
        d_value,
        d_output_weight,
        d_ffn_norm,
        d_router,
        d_gate,
        d_up,
        d_down,
    )


def solution(mesh):
    return jax.shard_map(
        per_device,
        mesh=mesh,
        in_specs=(
            P(("expert", "shard"), None),
            P("expert", "shard"),
            P(("expert", "shard"), None),
            P("shard"),
            P("shard", None),
            P("shard", None),
            P("shard", None),
            P(None, "shard"),
            P("shard"),
            P("shard", None),
            P("expert", "shard", None),
            P("expert", "shard", None),
            P("expert", None, "shard"),
            P(("expert", "shard"), None),
        ),
        out_specs=(
            P(("expert", "shard"), None),
            P(("expert", "shard"), None),
            P("shard"),
            P("shard", None),
            P("shard", None),
            P("shard", None),
            P(None, "shard"),
            P("shard"),
            P("shard", None),
            P("expert", "shard", None),
            P("expert", "shard", None),
            P("expert", None, "shard"),
        ),
        check_vma=False,
    )
```

profile of v0, /device:TPU:1, one launch (start us, length us, event | category | flops | bytes accessed | tf_op | source)
XLA Modules:
  0.0 955.9 jit_solution(5249237600901788139)
XLA Ops:
  9.4 8.8 all-gather.1
  19.4 16.6 %all-gather.13.cloned.1.call-done = bf16[1024,512]{1,0:T(8,128)(2,1)} async-done(((bf16[256,512]{1,0:T(8,128)(2,1)}), bf16[1024,512]{1,0:T(8,128)(2,1)}) %all-gather.13.cloned.1.call-update) | async-done | bytes 1048592 | tf_op jit(solution)/shard_map/all_gather | solution.py:59
  36.0 2.6 convolution_convert_fusion.9
  39.5 22.5 %all-gather.17.cloned.1.call-done = bf16[1024,512]{1,0:T(8,128)(2,1)} async-done(((bf16[256,512]{1,0:T(8,128)(2,1)}), bf16[1024,512]{1,0:T(8,128)(2,1)}) %all-gather.17.cloned.1.call-update) | async-done | bytes 1048592 | tf_op jit(solution)/shard_map/all_gather | solution.py:58
  62.0 2.0 fusion.85
  66.0 9.1 reduce-window.6
  76.2 7.2 all-gather.2
  83.4 5.9 all-gather
  91.2 31.1 %all-gather.21.cloned.1.call-done = bf16[1024,1024]{1,0:T(8,128)(2,1)} async-done(((bf16[256,1024]{1,0:T(8,128)(2,1)}), bf16[1024,1024]{1,0:T(8,128)(2,1)}) %all-gather.21.cloned.1.call-update) | async-done | bytes 2097168 | tf_op jit(solution)/shard_map/all_gather | solution.py:57
  122.2 2.6 fusion.83
  125.0 24.3 %all-gather.19.cloned.1.call-done = bf16[1024,512]{0,1:T(8,128)(2,1)} async-done(((bf16[256,512]{0,1:T(8,128)(2,1)}), bf16[1024,512]{0,1:T(8,128)(2,1)}) %all-gather.19.cloned.1.call-update) | async-done | bytes 1048592 | tf_op jit(solution)/shard_map/all_gather | solution.py:86
  149.3 13.6 %fusion.2 = f32[256,8,2,1024]{0,3,2,1:T(8,128)} fusion(pred[256,1024]{0,1:T(8,128)(4,1)S(1)} %fusion.62, bf16[1024,8,64,1]{0,2,3,1:T(8,128)(2,1)} %bitcast.190, bf16[256,8,2,32]{0,3,2,1:T(8,128)(2,1)S(1)} %bitcast.194, bf16[256,8,2,32]{0,3,2,1:T(8,128)(2,1)S(1)} %bitcast.192), kind=kOutput, calls=%fused_computation.8 | convolution fusion | flops 1096815616 | bytes 18612224 | tf_op jit(solution)/shard_map/reduce_sum | solution.py:199
  163.0 7.6 fusion.41
  170.6 15.8 %all-gather.23.cloned.1.call-done = bf16[1024,1024]{1,0:T(8,128)(2,1)} async-done(((bf16[1024,256]{1,0:T(8,128)(2,1)}), bf16[1024,1024]{1,0:T(8,128)(2,1)}) %all-gather.23.cloned.1.call-update) | async-done | bytes 2097168 | tf_op jit(solution)/shard_map/all_gather | solution.py:60
  186.4 2.4 multiply_reduce_fusion.3
  189.0 27.8 %scatter_custom_fusion = bf16[2304,1024]{1,0:T(8,128)(2,1)} fusion(s32[2048]{0:T(1024)S(1)} %get-tuple-element.50, bf16[256,1024]{1,0:T(8,128)(2,1)S(1)} %multiply_convert_fusion.3, s32[2048]{0:T(1024)S(1)} %get-tuple-element.49, bf16[]{:T(256)} %constant.51.clone.1), kind=kCustom, calls=%fused_computation.34 | custom fusion | bytes 4718594
  216.8 8.7 all-to-all-start
  227.5 10.2 %all_gather.58 = bf16[1024,32]{0,1:T(8,128)(2,1)S(1)} all-gather(bf16[256,32]{0,1:T(8,128)(2,1)S(1)} %copy-done.29), channel_id=1, replica_groups=mesh['expert'=32,'shard'=4] {'shard'}, dimensions={0}, use_global_device_ids=true | all-gather | bytes 81920 | tf_op jit(solution)/shard_map/all_gather | solution.py:62
  241.8 13.6 %scatter_custom_fusion.1 = bf16[2304,1024]{1,0:T(8,128)(2,1)} fusion(s32[2048]{0:T(1024)} %copy-done.33, f32[256,1024]{1,0:T(8,128)S(1)} %convert_element_type.260, f32[2048]{0:T(1024)} %div.57, bf16[]{:T(256)} %constant.51.clone.1), kind=kCustom, calls=%fused_computation.33 | custom fusion | flops 4194304 | bytes 5775872
  255.4 25.9 %all-to-all-done = bf16[32,72,1024]{2,1,0:T(8,128)(2,1)} async-done(((bf16[32,72,1024]{2,1,0:T(8,128)(2,1)}), bf16[32,72,1024]{2,1,0:T(8,128)(2,1)}, u32[]{:S(2)}, u32[]{:S(2)}) %all-to-all-start) | async-done | bytes 4718624 | tf_op jit(solution)/shard_map/all_to_all | solution.py:228
  281.3 8.7 all-to-all-start.2
  291.6 7.4 fusion.56
  299.0 17.5 %all-gather.25.cloned.1.call-done = bf16[1,1024,512]{2,1,0:T(8,128)(2,1)} async-done(((bf16[1,256,512]{2,1,0:T(8,128)(2,1)}), bf16[1,1024,512]{2,1,0:T(8,128)(2,1)}) %all-gather.25.cloned.1.call-update) | async-done | bytes 1048592 | tf_op jit(solution)/shard_map/all_gather | solution.py:63
  316.4 7.4 fusion.60
  323.8 20.6 %all-gather.29.cloned.1.call-done = bf16[1,512,1024]{2,1,0:T(8,128)(2,1)} async-done(((bf16[1,512,256]{2,1,0:T(8,128)(2,1)}), bf16[1,512,1024]{2,1,0:T(8,128)(2,1)}) %all-gather.29.cloned.1.call-update) | async-done | bytes 1048592 | tf_op jit(solution)/shard_map/all_gather | solution.py:65
  345.9 12.4 %multiply_convert_fusion = (bf16[2304,512]{1,0:T(8,128)(2,1)}, bf16[2304,512]{1,0:T(8,128)(2,1)}, bf16[2304,512]{1,0:T(8,128)(2,1)S(1)}) fusion(f32[2304,512]{1,0:T(8,128)} %fusion.60, f32[2304,512]{1,0:T(8,128)} %fusion.56, bf16[2304,1024]{1,0:T(8,128)(2,1)} %bitcast.31, bf16[1,512,1024]{2,1,0:T(8,128)(2,1)} %all-gather.29.cloned.1.call-done), kind=kOutput, calls=%fused_computation.28 | convolution fusion | flops 2433613824 | bytes 22282240 | tf_op jit(solution)/shard_map/nd,fd->nf/dot_general | solution.py:266
  358.3 4.2 convolution_convert_fusion
  362.5 9.3 all-to-all-start.1
  371.9 4.7 fusion.58
  376.6 4.4 add_convert_fusion
  381.1 46.4 %all-to-all-done.1 = bf16[32,72,1024]{2,1,0:T(8,128)(2,1)} async-done(((bf16[32,72,1024]{2,1,0:T(8,128)(2,1)}), bf16[32,72,1024]{2,1,0:T(8,128)(2,1)}, u32[]{:S(2)}, u32[]{:S(2)}) %all-to-all-start.1) | async-done | bytes 4718624 | tf_op jit(solution)/shard_map/all_to_all | solution.py:243
  427.5 8.8 all-to-all-start.3
  436.3 40.8 %gather_fusion = bf16[2048,1024]{1,0:T(8,128)(2,1)} fusion(bf16[32,72,1024]{2,1,0:T(8,128)(2,1)} %all-to-all-done.1, s32[2048]{0:T(1024)S(1)} %bitcast.170), kind=kCustom, calls=%fused_computation.1 | custom fusion | bytes 8404992 | tf_op jit(solution)/shard_map/gather | solution.py:245
  477.2 6.2 fusion.12
  486.5 5.6 all-to-all-done.3
  492.1 40.7 %gather_fusion.1 = bf16[2048,1024]{1,0:T(8,128)(2,1)} fusion(bf16[32,72,1024]{2,1,0:T(8,128)(2,1)} %all-to-all-done.3, s32[2048]{0:T(1024)S(1)} %bitcast.171), kind=kCustom, calls=%fused_computation.2 | custom fusion | bytes 8404992 | tf_op jit(solution)/shard_map/gather | solution.py:284
  532.9 5.6 convert_reduce_fusion
  542.2 9.6 %bitcast_convert_fusion = bf16[8,64,1024]{2,1,0:T(8,128)(2,1)} fusion(bf16[256,8,2,64]{0,3,2,1:T(8,128)(2,1)S(1)} %bitcast.178, f32[256,8,2,1024]{0,3,2,1:T(8,128)} %fusion.2), kind=kOutput, calls=%fused_computation.44 | convolution fusion | flops 541589504 | bytes 18350080 | tf_op jit(solution)/shard_map/qkaz,qkay->zky/dot_general | solution.py:345
  552.2 8.7 fusion.5
  560.9 4.8 bitcast_convert_fusion.1
  565.7 6.7 fusion.40
  572.5 6.8 fusion.39
  579.4 6.7 fusion.38
  586.3 2.8 convolution_convert_fusion.6
  589.1 11.1 %reduce-scatter.11.cloned.1.call-done = bf16[256,512]{0,1:T(8,128)(2,1)} async-done(((bf16[1024,512]{0,1:T(8,128)(2,1)}), bf16[256,512]{0,1:T(8,128)(2,1)}) %reduce-scatter.11.cloned.1.call-update) | async-done | bytes 262160 | tf_op jit(solution)/shard_map/reduce_scatter | solution.py:371
  603.0 2.1 convolution_convert_fusion.1
  605.4 5.0 fusion.89
  610.6 2.2 convolution_convert_fusion.2
  614.1 11.6 %reduce-scatter.29.cloned.1.call-done = bf16[1,512,256]{2,1,0:T(8,128)(2,1)} async-done(((bf16[1,512,1024]{2,1,0:T(8,128)(2,1)}), bf16[1,512,256]{2,1,0:T(8,128)(2,1)}) %reduce-scatter.29.cloned.1.call-update) | async-done | bytes 262160 | tf_op jit(solution)/shard_map/reduce_scatter | solution.py:296
  627.5 24.0 %reduce-scatter.27.cloned.1.call-done = bf16[1,256,512]{2,1,0:T(8,128)(2,1)} async-done(((bf16[1,1024,512]{2,1,0:T(8,128)(2,1)}), bf16[1,256,512]{2,1,0:T(8,128)(2,1)}) %reduce-scatter.27.cloned.1.call-update) | async-done | bytes 262160 | tf_op jit(solution)/shard_map/reduce_scatter | solution.py:293
  651.6 1.8 convert_element_type.301
  653.4 23.7 %reduce-scatter.25.cloned.1.call-done = bf16[1,256,512]{2,1,0:T(8,128)(2,1)} async-done(((bf16[1,1024,512]{2,1,0:T(8,128)(2,1)}), bf16[1,256,512]{2,1,0:T(8,128)(2,1)}) %reduce-scatter.25.cloned.1.call-update) | async-done | bytes 262160 | tf_op jit(solution)/shard_map/reduce_scatter | solution.py:290
  679.8 2.3 fusion.90
  682.2 2.7 convolution_add_fusion.2
  684.9 17.9 %reduce-scatter.19.cloned.1.call-done = bf16[256,512]{1,0:T(8,128)(2,1)} async-done(((bf16[1024,512]{1,0:T(8,128)(2,1)}), bf16[256,512]{1,0:T(8,128)(2,1)}) %reduce-scatter.19.cloned.1.call-update) | async-done | bytes 262160 | tf_op jit(solution)/shard_map/reduce_scatter | solution.py:442
  702.8 26.1 %reduce-scatter.17.cloned.1.call-done = bf16[256,512]{1,0:T(8,128)(2,1)} async-done(((bf16[1024,512]{1,0:T(8,128)(2,1)}), bf16[256,512]{1,0:T(8,128)(2,1)}) %reduce-scatter.17.cloned.1.call-update) | async-done | bytes 262160 | tf_op jit(solution)/shard_map/reduce_scatter | solution.py:439
  728.9 33.2 %reduce-scatter.21.cloned.1.call-done = bf16[1024,256]{1,0:T(8,128)(2,1)} async-done(((bf16[1024,1024]{1,0:T(8,128)(2,1)}), bf16[1024,256]{1,0:T(8,128)(2,1)}) %reduce-scatter.21.cloned.1.call-update) | async-done | bytes 524304 | tf_op jit(solution)/shard_map/reduce_scatter | solution.py:445
  762.1 31.7 %reduce-scatter.15.cloned.1.call-done = bf16[256,1024]{1,0:T(8,128)(2,1)} async-done(((bf16[1024,1024]{1,0:T(8,128)(2,1)}), bf16[256,1024]{1,0:T(8,128)(2,1)}) %reduce-scatter.15.cloned.1.call-update) | async-done | bytes 524304 | tf_op jit(solution)/shard_map/reduce_scatter | solution.py:436
  793.9 2.3 fusion.50
  796.1 6.5 all-reduce.4
  802.8 11.8 %reduce-scatter.23.cloned.1.call-done = bf16[256,32]{0,1:T(8,128)(2,1)} async-done(((bf16[1024,32]{0,1:T(8,128)(2,1)}), bf16[256,32]{0,1:T(8,128)(2,1)}) %reduce-scatter.23.cloned.1.call-update) | async-done | bytes 16400 | tf_op jit(solution)/shard_map/reduce_scatter | solution.py:451
  814.6 123.5 %all-reduce.2 = (bf16[256]{0:T(256)(128)(2,1)S(1)}, bf16[256]{0:T(256)(128)(2,1)S(1)}, bf16[256,32]{0,1:T(8,128)(2,1)S(1)}) all-reduce(bf16[256]{0:T(256)(128)(2,1)S(1)} %dynamic-slice.1, bf16[256]{0:T(256)(128)(2,1)S(1)} %dynamic-slice.3, ...), channel_id=1, replica_groups=mesh['expert'=32,'shard'=4] {'expert'}, use_global_device_ids=true, to_apply=%region_22.23 | all-reduce | flops 8704 | bytes 34816 | tf_op jit(solution)/shard_map/psum | solution.py:456
  941.0 2.1 convert_element_type.285
  946.7 2.1 convert_element_type.291
  (202 shorter events, 40.9 us)
Async XLA Ops:
  7.2 58.2 %copy-start.24 = (s32[256,8]{0,1:T(8,128)S(1)}, s32[256,8]{0,1:T(8,128)}, u32[]{:S(2)}) copy-start(s32[256,8]{0,1:T(8,128)} %param.16) | copy-start | bytes 24580
  7.2 58.7 %copy-start.34 = (s32[1,256]{1,0:T(1,128)S(1)}, s32[1,256]{1,0:T(1,128)}, u32[]{:S(2)}) copy-start(s32[1,256]{1,0:T(1,128)} %param.15) | copy-start | bytes 3076
  7.2 28.8 %all-gather.13.cloned.1.call-start = ((), (), s32[]{:S(2)}) async-start(), calls=%async_computation.14 | async-start | bytes 1310720 | tf_op jit(solution)/shard_map/all_gather | solution.py:59
  7.9 54.1 %all-gather.17.cloned.1.call-start = ((), (), s32[]{:S(2)}) async-start(), calls=%async_computation.16 | async-start | bytes 1310720 | tf_op jit(solution)/shard_map/all_gather | solution.py:58
  8.7 81.0 %all-gather.15.cloned.1.call-start = ((), (), s32[]{:S(2)}) async-start(), calls=%async_computation.15 | async-start | bytes 1310720 | tf_op jit(solution)/shard_map/all_gather | solution.py:87
  18.2 104.0 %copy-start.20 = (f32[4,1,256]{2,1,0:T(1,128)}, f32[4,1,256]{2,1,0:T(1,128)S(1)}, u32[]{:S(2)}) copy-start(f32[4,1,256]{2,1,0:T(1,128)S(1)} %convert_element_type.307) | copy-start | bytes 12292
  19.4 102.8 %copy-start.27 = (f32[256]{0:T(256)}, f32[256]{0:T(256)S(1)}, u32[]{:S(2)}) copy-start(f32[256]{0:T(256)S(1)} %add_rsqrt_fusion.1) | copy-start | bytes 3076
  36.0 39.9 %copy-start.36 = (s32[2]{0:T(128)S(1)}, s32[2]{0:T(128)}, u32[]{:S(2)}) copy-start(s32[2]{0:T(128)} %constant.67) | copy-start | bytes 28
  36.0 40.0 %copy-start.35 = (s32[2]{0:T(128)S(1)}, s32[2]{0:T(128)}, u32[]{:S(2)}) copy-start(s32[2]{0:T(128)} %constant.64) | copy-start | bytes 28
  38.6 37.5 %copy-start.39 = (bf16[256]{0:T(256)(128)(2,1)S(1)}, bf16[256]{0:T(256)(128)(2,1)}, u32[]{:S(2)}) copy-start(bf16[256]{0:T(256)(128)(2,1)} %param.22) | copy-start | bytes 1540
  38.7 83.6 %all-gather.21.cloned.1.call-start = ((), (), s32[]{:S(2)}) async-start(), calls=%async_computation.18 | async-start | bytes 2621440 | tf_op jit(solution)/shard_map/all_gather | solution.py:57
  39.2 110.1 %all-gather.19.cloned.1.call-start = ((), (), s32[]{:S(2)}) async-start(), calls=%async_computation.17 | async-start | bytes 1310720 | tf_op jit(solution)/shard_map/all_gather | solution.py:86
  39.5 85.3 %copy-start.14 = (f32[256,32]{0,1:T(8,128)}, f32[256,32]{0,1:T(8,128)S(1)}, u32[]{:S(2)}) copy-start(f32[256,32]{0,1:T(8,128)S(1)} %get-tuple-element.43) | copy-start | bytes 98308
  39.5 85.3 %copy-start.16 = (f32[256,32]{0,1:T(8,128)}, f32[256,32]{0,1:T(8,128)S(1)}, u32[]{:S(2)}) copy-start(f32[256,32]{0,1:T(8,128)S(1)} %get-tuple-element.44) | copy-start | bytes 98308
  39.5 82.7 %copy-start.1 = (bf16[256,1024]{1,0:T(8,128)(2,1)S(1)}, bf16[256,1024]{1,0:T(8,128)(2,1)}, u32[]{:S(2)}) copy-start(bf16[256,1024]{1,0:T(8,128)(2,1)} %param.14) | copy-start | bytes 1572868
  64.8 121.5 %all-gather.23.cloned.1.call-start = ((), (), s32[]{:S(2)}) async-start(), calls=%async_computation.19 | async-start | bytes 2621440 | tf_op jit(solution)/shard_map/all_gather | solution.py:60
  83.4 105.4 %copy-start.25 = (f32[4,1,256]{2,1,0:T(1,128)}, f32[4,1,256]{2,1,0:T(1,128)S(1)}, u32[]{:S(2)}) copy-start(f32[4,1,256]{2,1,0:T(1,128)S(1)} %convert_element_type.308) | copy-start | bytes 12292
  89.4 99.6 %copy-start.33 = (s32[2048]{0:T(1024)}, s32[2048]{0:T(1024)S(1)}, u32[]{:S(2)}) copy-start(s32[2048]{0:T(1024)S(1)} %get-tuple-element.50) | copy-start | bytes 24580
  91.1 71.8 %copy-start.4 = (bf16[1024,512]{0,1:T(8,128)(2,1)}, bf16[1024,512]{0,1:T(8,128)(2,1)S(1)}, u32[]{:S(2)}) copy-start(bf16[1024,512]{0,1:T(8,128)(2,1)S(1)} %copy.86) | copy-start | bytes 3145732
  125.0 37.9 %copy-start.12 = (bf16[256,16,32]{0,2,1:T(8,128)(2,1)}, bf16[256,16,32]{0,2,1:T(8,128)(2,1)S(1)}, u32[]{:S(2)}) copy-start(bf16[256,16,32]{0,2,1:T(8,128)(2,1)S(1)} %get-tuple-element.33) | copy-start | bytes 786436
  188.8 28.0 %copy-start.31 = (f32[256]{0:T(256)}, f32[256]{0:T(256)S(1)}, u32[]{:S(2)}) copy-start(f32[256]{0:T(256)S(1)} %add_rsqrt_fusion) | copy-start | bytes 3076
  189.0 27.8 %copy-start.7 = (bf16[256,1024]{1,0:T(8,128)(2,1)}, bf16[256,1024]{1,0:T(8,128)(2,1)S(1)}, u32[]{:S(2)}) copy-start(bf16[256,1024]{1,0:T(8,128)(2,1)S(1)} %multiply_convert_fusion.3) | copy-start | bytes 1572868
  216.8 10.7 %copy-start.29 = (bf16[256,32]{0,1:T(8,128)(2,1)S(1)}, bf16[256,32]{0,1:T(8,128)(2,1)}, u32[]{:S(2)}) copy-start(bf16[256,32]{0,1:T(8,128)(2,1)} %param.23) | copy-start | bytes 49156
  216.8 64.5 %all-to-all-start = ((bf16[32,72,1024]{2,1,0:T(8,128)(2,1)}), bf16[32,72,1024]{2,1,0:T(8,128)(2,1)}, u32[]{:S(2)}, u32[]{:S(2)}) async-start(bf16[32,72,1024]{2,1,0:T(8,128)(2,1)} %bitcast.173), calls=%async_computation | async-start | bytes 9437184 | tf_op jit(solution)/shard_map/all_to_all | solution.py:228
  225.5 66.0 %all-gather.27.cloned.1.call-start = ((), (), s32[]{:S(2)}) async-start(), calls=%async_computation.21 | async-start | bytes 1310720 | tf_op jit(solution)/shard_map/all_gather | solution.py:64
  281.3 64.6 %all-to-all-start.2 = ((bf16[32,72,1024]{2,1,0:T(8,128)(2,1)}), bf16[32,72,1024]{2,1,0:T(8,128)(2,1)}, u32[]{:S(2)}, u32[]{:S(2)}) async-start(bf16[32,72,1024]{2,1,0:T(8,128)(2,1)} %bitcast.172), calls=%async_computation.2 | async-start | bytes 9437184 | tf_op jit(solution)/shard_map/all_to_all | solution.py:263
  290.0 26.4 %all-gather.25.cloned.1.call-start = ((), (), s32[]{:S(2)}) async-start(), calls=%async_computation.20 | async-start | bytes 1310720 | tf_op jit(solution)/shard_map/all_gather | solution.py:63
  290.8 53.6 %all-gather.29.cloned.1.call-start = ((), (), s32[]{:S(2)}) async-start(), calls=%async_computation.22 | async-start | bytes 1310720 | tf_op jit(solution)/shard_map/all_gather | solution.py:65
  345.9 12.4 %copy-start.38 = (bf16[1,512,1024]{2,1,0:T(8,128)(2,1)S(1)}, bf16[1,512,1024]{2,1,0:T(8,128)(2,1)}, u32[]{:S(2)}) copy-start(bf16[1,512,1024]{2,1,0:T(8,128)(2,1)} %all-gather.29.cloned.1.call-done) | copy-start | bytes 3145732
  358.3 4.2 copy-start.42
  362.5 65.0 %all-to-all-start.1 = ((bf16[32,72,1024]{2,1,0:T(8,128)(2,1)}), bf16[32,72,1024]{2,1,0:T(8,128)(2,1)}, u32[]{:S(2)}, u32[]{:S(2)}) async-start(bf16[32,72,1024]{2,1,0:T(8,128)(2,1)} %bitcast.182), calls=%async_computation.1 | async-start | bytes 9437184 | tf_op jit(solution)/shard_map/all_to_all | solution.py:243
  371.9 4.8 copy-start.37
  371.9 4.8 copy-start.41
  427.5 64.6 %all-to-all-start.3 = ((bf16[32,72,1024]{2,1,0:T(8,128)(2,1)}), bf16[32,72,1024]{2,1,0:T(8,128)(2,1)}, u32[]{:S(2)}, u32[]{:S(2)}) async-start(bf16[32,72,1024]{2,1,0:T(8,128)(2,1)} %bitcast.181), calls=%async_computation.3 | async-start | bytes 9437184 | tf_op jit(solution)/shard_map/all_to_all | solution.py:282
  436.3 150.0 %reduce-scatter.13.cloned.1.call-start = ((), (), s32[]{:S(2)}) async-start(), calls=%async_computation.24 | async-start | bytes 1310720 | tf_op jit(solution)/shard_map/reduce_scatter | solution.py:379
  486.5 52.0 %copy-start.22 = (bf16[256,32]{0,1:T(8,128)(2,1)}, bf16[256,32]{0,1:T(8,128)(2,1)S(1)}, u32[]{:S(2)}) copy-start(bf16[256,32]{0,1:T(8,128)(2,1)S(1)} %select_reduce_fusion) | copy-start | bytes 49156
  532.8 5.6 copy-start.19
  532.8 5.6 copy-start.26
  532.8 5.6 copy-start.32
  532.8 6.2 copy-start.9
  532.8 6.2 copy-start.10
  538.5 2.7 copy-start.5
  542.2 9.8 %copy-start.6 = (bf16[256,1024]{0,1:T(8,128)(2,1)}, bf16[256,1024]{0,1:T(8,128)(2,1)S(1)}, u32[]{:S(2)}) copy-start(bf16[256,1024]{0,1:T(8,128)(2,1)S(1)} %copy.99) | copy-start | bytes 1572868
  551.8 48.4 %reduce-scatter.11.cloned.1.call-start = ((), (), s32[]{:S(2)}) async-start(), calls=%async_computation.23 | async-start | bytes 1310720 | tf_op jit(solution)/shard_map/reduce_scatter | solution.py:371
  560.9 4.8 copy-start
  565.7 60.1 %reduce-scatter.29.cloned.1.call-start = ((), (), s32[]{:S(2)}) async-start(), calls=%async_computation.32 | async-start | bytes 1310720 | tf_op jit(solution)/shard_map/reduce_scatter | solution.py:296
  572.5 79.1 %reduce-scatter.27.cloned.1.call-start = ((), (), s32[]{:S(2)}) async-start(), calls=%async_computation.31 | async-start | bytes 1310720 | tf_op jit(solution)/shard_map/reduce_scatter | solution.py:293
  579.3 6.9 copy-start.21
  579.3 6.9 copy-start.28
  579.3 21.9 %copy-start.15 = (f32[256,32]{0,1:T(8,128)S(1)}, f32[256,32]{0,1:T(8,128)}, u32[]{:S(2)}) copy-start(f32[256,32]{0,1:T(8,128)} %copy-done.14) | copy-start | bytes 98308
  579.4 21.9 %copy-start.17 = (f32[256,32]{0,1:T(8,128)S(1)}, f32[256,32]{0,1:T(8,128)}, u32[]{:S(2)}) copy-start(f32[256,32]{0,1:T(8,128)} %copy-done.16) | copy-start | bytes 98308
  579.4 97.7 %reduce-scatter.25.cloned.1.call-start = ((), (), s32[]{:S(2)}) async-start(), calls=%async_computation.30 | async-start | bytes 1310720 | tf_op jit(solution)/shard_map/reduce_scatter | solution.py:290
  586.1 16.8 %copy-start.3 = (f32[256,1024]{1,0:T(8,128)S(1)}, f32[256,1024]{1,0:T(8,128)}, u32[]{:S(2)}) copy-start(f32[256,1024]{1,0:T(8,128)} %copy-done.2) | copy-start | bytes 3145732
  586.2 116.6 %reduce-scatter.19.cloned.1.call-start = ((), (), s32[]{:S(2)}) async-start(), calls=%async_computation.27 | async-start | bytes 1310720 | tf_op jit(solution)/shard_map/reduce_scatter | solution.py:442
  589.1 139.9 %reduce-scatter.17.cloned.1.call-start = ((), (), s32[]{:S(2)}) async-start(), calls=%async_computation.26 | async-start | bytes 1310720 | tf_op jit(solution)/shard_map/reduce_scatter | solution.py:439
  601.3 4.1 copy-start.11
  602.9 159.2 %reduce-scatter.21.cloned.1.call-start = ((), (), s32[]{:S(2)}) async-start(), calls=%async_computation.28 | async-start | bytes 2621440 | tf_op jit(solution)/shard_map/reduce_scatter | solution.py:445
  605.1 188.7 %reduce-scatter.15.cloned.1.call-start = ((), (), s32[]{:S(2)}) async-start(), calls=%async_computation.25 | async-start | bytes 2621440 | tf_op jit(solution)/shard_map/reduce_scatter | solution.py:436
  610.4 2.5 copy-start.40
  610.5 68.4 %copy-start.8 = (bf16[256,1024]{1,0:T(8,128)(2,1)S(1)}, bf16[256,1024]{1,0:T(8,128)(2,1)}, u32[]{:S(2)}) copy-start(bf16[256,1024]{1,0:T(8,128)(2,1)} %copy-done.7) | copy-start | bytes 1572868
  610.6 68.4 %copy-start.23 = (bf16[256,32]{0,1:T(8,128)(2,1)S(1)}, bf16[256,32]{0,1:T(8,128)(2,1)}, u32[]{:S(2)}) copy-start(bf16[256,32]{0,1:T(8,128)(2,1)} %copy-done.22) | copy-start | bytes 49156
  612.8 201.8 %reduce-scatter.23.cloned.1.call-start = ((), (), s32[]{:S(2)}) async-start(), calls=%async_computation.29 | async-start | bytes 81920 | tf_op jit(solution)/shard_map/reduce_scatter | solution.py:451
  678.9 115.0 %copy-start.13 = (bf16[256,512]{0,1:T(8,128)(2,1)S(1)}, bf16[256,512]{0,1:T(8,128)(2,1)}, u32[]{:S(2)}) copy-start(bf16[256,512]{0,1:T(8,128)(2,1)} %reduce-scatter.13.cloned.1.call-done) | copy-start | bytes 786436
  679.8 261.2 %all-reduce.7.cloned.1.call-start = ((), (), s32[]{:S(2)}) async-start(), calls=%async_computation.33 | async-start | bytes 3145728 | tf_op jit(solution)/shard_map/psum | solution.py:457
  (3 other events, 3.0 us)
Sparse Core Ops, SparseCore 0:
  9.7 26.2 all-gather.12
  37.7 24.2 all-gather.16
  64.2 24.2 all-gather.14
  90.1 32.0 all-gather.20
  124.3 25.0 all-gather.18
  150.9 35.4 all-gather.22
  228.0 23.7 all-gather.26
  292.6 23.8 all-gather.24
  318.1 26.2 all-gather.28
  551.9 21.8 reduce-scatter.12
  577.0 23.2 reduce-scatter.10
  602.5 23.2 reduce-scatter.28
  628.3 23.2 reduce-scatter.26
  653.8 23.2 reduce-scatter.24
  679.5 23.2 reduce-scatter.18
  705.6 23.2 reduce-scatter.16
  731.3 30.8 reduce-scatter.20
  764.4 29.3 reduce-scatter.14
  796.9 17.7 reduce-scatter.22
  818.2 108.3 all-reduce.6
where the time goes:
time: 971 us; the launch traced here: 956 us
  waiting for transfers between devices  424 us (44%)
  blocking collectives  162 us (17%)
  matrix products  139 us (14%)
  local copies, waits for them, and re-layouts  118 us (12%)
  other arithmetic  60.8 us (6%)
  starting transfers between devices  37 us (4%)
  between operations  16 us (2%)
    psum x1, blocking collectives, per_device(): lax.psum(partial_sums[0].astype(jnp.bfloat16), 'expert').astype(jnp.float32)  123 us
    all_to_all x1, waiting for transfers between devices, per_device(): lax.all_to_all(result, 'expert', split_axis=0, concat_axis=0, tiled=True)  46.4 us
    gather x1, local copies, waits for them, and re-layouts, per_device(): returned[flat_ids, slot_pos].astype(single_float)  40.8 us
    gather x1, local copies, waits for them, and re-layouts, per_device(): back_grads[flat_ids, slot_pos].astype(single_float)  40.7 us
    reduce_scatter x1, waiting for transfers between devices, per_device(): lax.psum_scatter(dense_terms[4].astype(jnp.bfloat16), 'shard', scatter_di...  33.2 us
    reduce_scatter x1, waiting for transfers between devices, per_device(): lax.psum_scatter(dense_terms[1].astype(jnp.bfloat16), 'shard', scatter_di...  31.7 us
    all_gather x1, waiting for transfers between devices, gather_weights(): lax.all_gather(weights[1], 'shard', axis=0, tiled=True)  31.1 us
    unnamed x93, local copies, waits for them, and re-layouts  31.1 us
  transfers between devices with their start and end apart: 24, of which 20 were waited for; matrix products, arithmetic and copies ran while one was open for 21% of the time, Pallas kernels for 0%

commit v1 on v0

v1 whole, which is shorter than its diff:
```python
import functools

import jax
import jax.numpy as jnp
from jax import lax
from jax.experimental import pallas as pl
from jax.experimental.pallas import tpu as pltpu
from jax.sharding import PartitionSpec as P

D = 1024
NH = 16
NKV = 8
HD = 64
FF = 512
TOPK = 8
NE = 32
NS = 4
T = 256
CAP = 72
SLOTS = NE * CAP
GC = 512
EPS = 1e-05
BASE = 10000.0
F32 = jnp.float32
BF = jnp.bfloat16
MESH = pl.DeviceIdType.MESH
ANY = pl.BlockSpec(memory_space=pl.ANY)
VM = pl.BlockSpec(memory_space=pltpu.VMEM)
DMA = pltpu.SemaphoreType.DMA
SMALL = 64


def nn(a, b):
    return lax.dot_general(a, b, (((1,), (0,)), ((), ())), preferred_element_type=F32)


def nt(a, b):
    return lax.dot_general(a, b, (((1,), (1,)), ((), ())), preferred_element_type=F32)


def tn(a, b):
    return lax.dot_general(a, b, (((0,), (0,)), ((), ())), preferred_element_type=F32)


def sds(shape, dtype):
    return jax.ShapeDtypeStruct(shape, dtype)


def plain(kernel, outs, *args, name, flops=0, moved=0, **kw):
    return pl.pallas_call(
        kernel,
        out_shape=outs,
        in_specs=[VM] * len(args),
        out_specs=jax.tree.map(lambda _: VM, outs),
        compiler_params=pltpu.CompilerParams(vmem_limit_bytes=56 << 20),
        cost_estimate=pl.CostEstimate(flops=flops, bytes_accessed=moved, transcendentals=0),
        name=name,
        **kw,
    )(*args)


def gather_front_kernel(x, wq, wk, wv, small, xo, wo, so, sx, rx, sw, rw, sf, rf, sm, rm, ls):
    i, s = lax.axis_index("expert"), lax.axis_index("shard")
    core = lax.rem(i, 2)
    sib = i + 1 - 2 * core
    right, left, far = lax.rem(s + 1, NS), lax.rem(s + 3, NS), lax.rem(s + 2, NS)
    bar = pltpu.get_barrier_semaphore()
    for p in (right, left, far):
        pl.semaphore_signal(bar, inc=1, device_id=(i, p), device_id_type=MESH)
    pl.semaphore_signal(bar, inc=1, device_id=(sib, s), device_id_type=MESH)
    pl.semaphore_wait(bar, 4)

    def put(src, dst, a, b, dev):
        c = pltpu.make_async_remote_copy(src, dst, a, b, device_id=dev, device_id_type=MESH)
        c.start()
        return c

    top, bot = pl.ds(0, T // 2), pl.ds(T // 2, T // 2)
    sends = []
    for k, p in ((0, right), (1, left), (2, far)):
        sends.append(put(small, so.at[s], sm.at[k], rm.at[k], (i, p)))
    half = pl.ds(core * (T // 2), T // 2)
    for k, p in ((0, right), (1, left), (2, far)):
        sends.append(put(wq.at[half, pl.ds(p * 256, 256)], wo.at[s, half, pl.ds(0, 256)], sw.at[k, 0], rw.at[k, 0], (i, p)))
        sends.append(put(wk.at[half, pl.ds(p * 128, 128)], wo.at[s, half, pl.ds(256, 128)], sw.at[k, 1], rw.at[k, 1], (i, p)))
        sends.append(put(wv.at[half, pl.ds(p * 128, 128)], wo.at[s, half, pl.ds(384, 128)], sw.at[k, 2], rw.at[k, 2], (i, p)))
    rt = put(x.at[top], xo.at[s, top], sx.at[0], rx.at[0], (i, right))
    lb = put(x.at[bot], xo.at[s, bot], sx.at[1], rx.at[1], (i, left))
    rb = put(x.at[bot], xo.at[s, bot], sx.at[2], rx.at[2], (i, right))
    lt = put(x.at[top], xo.at[s, top], sx.at[3], rx.at[3], (i, left))
    loc = [
        pltpu.make_async_copy(x, xo.at[s], ls.at[0]),
        pltpu.make_async_copy(small, so.at[s], ls.at[1]),
        pltpu.make_async_copy(wq.at[:, pl.ds(s * 256, 256)], wo.at[s, :, pl.ds(0, 256)], ls.at[2]),
        pltpu.make_async_copy(wk.at[:, pl.ds(s * 128, 128)], wo.at[s, :, pl.ds(256, 128)], ls.at[3]),
        pltpu.make_async_copy(wv.at[:, pl.ds(s * 128, 128)], wo.at[s, :, pl.ds(384, 128)], ls.at[4]),
    ]
    for c in loc:
        c.start()
    for k, src in ((0, left), (1, right), (2, far)):
        for j in range(3):
            sends[3 + 3 * k + j].wait_recv()
        sends.append(put(wo.at[src, half], wo.at[src, half], sf.at[k], rf.at[k], (sib, s)))
    rt.wait_recv()
    ft = put(xo.at[left, top], xo.at[left, top], sx.at[4], rx.at[4], (i, right))
    lb.wait_recv()
    fb = put(xo.at[right, bot], xo.at[right, bot], sx.at[5], rx.at[5], (i, left))
    for c in (rb, lt, ft, fb):
        c.wait_recv()
    for c in sends[:3]:
        c.wait_recv()
    for c in sends[12:]:
        c.wait_recv()
    for c in sends + [rt, lb, rb, lt, ft, fb]:
        c.wait_send()
    for c in loc:
        c.wait()


def gather_front(x, wq, wk, wv, small):
    return pl.pallas_call(
        gather_front_kernel,
        out_shape=(sds((NS, T, D), BF), sds((NS, T, GC), BF), sds((NS,) + small.shape, F32)),
        in_specs=[ANY] * 5,
        out_specs=(ANY, ANY, ANY),
        scratch_shapes=[DMA((6,)), DMA((6,)), DMA((3, 3)), DMA((3, 3)), DMA((3,)), DMA((3,)), DMA((3,)), DMA((3,)), DMA((5,))],
        compiler_params=pltpu.CompilerParams(collective_id=0, has_side_effects=True),
        cost_estimate=pl.CostEstimate(flops=0, bytes_accessed=90 << 20, transcendentals=0),
        name="gather_front",
    )(x, wq, wk, wv, small)


def swap_kernel(x, o, ss, rs, ls):
    i, s = lax.axis_index("expert"), lax.axis_index("shard")
    peers = [lax.rem(s + k, NS) for k in (2, 1, 3)]
    bar = pltpu.get_barrier_semaphore()
    for p in peers:
        pl.semaphore_signal(bar, inc=1, device_id=(i, p), device_id_type=MESH)
    pl.semaphore_wait(bar, 3)
    copies = []
    for k, p in enumerate(peers):
        c = pltpu.make_async_remote_copy(x.at[p], o.at[s], ss.at[k], rs.at[k], device_id=(i, p), device_id_type=MESH)
        c.start()
        copies.append(c)
    loc = pltpu.make_async_copy(x.at[s], o.at[s], ls)
    loc.start()
    for c in copies:
        c.wait()
    loc.wait()


def swap(x, cid):
    return pl.pallas_call(
        swap_kernel,
        out_shape=sds(x.shape, x.dtype),
        in_specs=[ANY],
        out_specs=ANY,
        scratch_shapes=[DMA((3,)), DMA((3,)), DMA],
        compiler_params=pltpu.CompilerParams(collective_id=cid, has_side_effects=True),
        cost_estimate=pl.CostEstimate(flops=0, bytes_accessed=30 << 20, transcendentals=0),
        name="swap%d" % cid,
    )(x)


def reduce_kernel(
    a, b, g, ao, bo, go,
    pa, pb, pg, ya, yb, yg, a1, b1, g1, xa, xb, xg, a2, b2, g2, za, zb, zg, a3, b3, ra, rb, rg, og,
    ss, rs, ls,
):
    i, s = lax.axis_index("expert"), lax.axis_index("shard")
    core = lax.rem(i, 2)
    sib = i + 1 - 2 * core
    xi, zi = lax.rem(lax.div(i, 2), 4), lax.div(i, 8)

    def at_x(q):
        return (zi * 8 + q * 2 + core, s)

    def at_z(q):
        return (q * 8 + xi * 2 + core, s)

    bar = pltpu.get_barrier_semaphore()
    pl.semaphore_signal(bar, inc=1, device_id=(sib, s), device_id_type=MESH)
    for k in (1, 2, 3):
        pl.semaphore_signal(bar, inc=1, device_id=(i, lax.rem(s + k, 4)), device_id_type=MESH)
        pl.semaphore_signal(bar, inc=1, device_id=at_x(lax.rem(xi + k, 4)), device_id_type=MESH)
        pl.semaphore_signal(bar, inc=1, device_id=at_z(lax.rem(zi + k, 4)), device_id_type=MESH)
    pl.semaphore_wait(bar, 10)
    count = [0]

    def put(src, dst, dev):
        n = count[0]
        count[0] += 1
        c = pltpu.make_async_remote_copy(src, dst, ss.at[n], rs.at[n], device_id=dev, device_id_type=MESH)
        c.start()
        return c

    mine, other = core, 1 - core
    c0 = [
        put(a.at[:, pl.ds(other * 128, 128), :], pa, (sib, s)),
        put(b.at[:, pl.ds(other * 512, 512), :], pb, (sib, s)),
        put(g.at[:, :, pl.ds(other * 128, 128)], pg, (sib, s)),
    ]
    for c in c0:
        c.wait()
    for p in range(NS):
        ya[p] = (a[p, pl.ds(mine * 128, 128), :].astype(F32) + pa[p].astype(F32)).astype(BF)
        yb[p] = (b[p, pl.ds(mine * 512, 512), :].astype(F32) + pb[p].astype(F32)).astype(BF)
    yg[...] = g[:, :, pl.ds(mine * 128, 128)] + pg[...]
    c1 = []
    for k in (2, 1, 3):
        p = lax.rem(s + k, 4)
        c1.append(put(ya.at[p], a1.at[s], (i, p)))
        c1.append(put(yb.at[p], b1.at[k - 1], (i, p)))
        c1.append(put(yg.at[p], g1.at[k - 1], (i, p)))
    a1[s] = ya[s]
    for c in c1:
        c.wait()
    xb[...] = (yb[s].astype(F32) + b1[0].astype(F32) + b1[1].astype(F32) + b1[2].astype(F32)).astype(BF)
    xg[...] = yg[s] + g1[0] + g1[1] + g1[2]
    c2 = []
    for k in (2, 1, 3):
        q = lax.rem(xi + k, 4)
        c2.append(put(a1.at[q], a2.at[k - 1], at_x(q)))
        c2.append(put(xb.at[pl.ds(q * 128, 128), :], b2.at[k - 1], at_x(q)))
        c2.append(put(xg.at[pl.ds(q * 16, 16), :], g2.at[k - 1], at_x(q)))
    for c in c2:
        c.wait()
    za[...] = (a1[xi].astype(F32) + a2[0].astype(F32) + a2[1].astype(F32) + a2[2].astype(F32)).astype(BF)
    zb[...] = (
        xb[pl.ds(xi * 128, 128), :].astype(F32) + b2[0].astype(F32) + b2[1].astype(F32) + b2[2].astype(F32)
    ).astype(BF)
    zg[...] = xg[pl.ds(xi * 16, 16), :] + g2[0] + g2[1] + g2[2]
    c3 = []
    for k in (2, 1, 3):
        q = lax.rem(zi + k, 4)
        c3.append(put(za.at[pl.ds(q * 32, 32), :], a3.at[k - 1], at_z(q)))
        c3.append(put(zb.at[pl.ds(q * 32, 32), :], b3.at[k - 1], at_z(q)))
        c3.append(put(zg, rg.at[k - 1], at_z(q)))
    for c in c3:
        c.wait()
    own = pl.ds(zi * 32, 32)
    ra[xi, own, :] = (za[own, :].astype(F32) + a3[0].astype(F32) + a3[1].astype(F32) + a3[2].astype(F32)).astype(BF)
    rb[xi, own, :] = (zb[own, :].astype(F32) + b3[0].astype(F32) + b3[1].astype(F32) + b3[2].astype(F32)).astype(BF)
    og[pl.ds(xi * 16, 16), :] = zg[...] + rg[0] + rg[1] + rg[2]
    c4 = []
    for k in (2, 1, 3):
        q = lax.rem(zi + k, 4)
        c4.append(put(ra.at[xi, own, :], ra.at[xi, own, :], at_z(q)))
        c4.append(put(rb.at[xi, own, :], rb.at[xi, own, :], at_z(q)))
    for c in c4:
        c.wait()
    c5 = []
    for k in (2, 1, 3):
        q = lax.rem(xi + k, 4)
        c5.append(put(ra.at[xi], ra.at[xi], at_x(q)))
        c5.append(put(rb.at[xi], rb.at[xi], at_x(q)))
        c5.append(put(og.at[pl.ds(xi * 16, 16), :], og.at[pl.ds(xi * 16, 16), :], at_x(q)))
    for c in c5:
        c.wait()
    ha, hb, hg = pl.ds(core * 128, 128), pl.ds(core * 4, 4), pl.ds(core * 128, 128)
    c6 = [
        put(ra, ao.at[:, ha, :], (sib, s)),
        put(rb, bo.at[hb], (sib, s)),
        put(og, go.at[:, hg], (sib, s)),
    ]
    loc = [
        pltpu.make_async_copy(ra, ao.at[:, ha, :], ls.at[0]),
        pltpu.make_async_copy(rb, bo.at[hb], ls.at[1]),
        pltpu.make_async_copy(og, go.at[:, hg], ls.at[2]),
    ]
    for c in loc:
        c.start()
    for c in c6 + loc:
        c.wait()


def reduce_dense(a, b, g):
    v = pltpu.VMEM
    return pl.pallas_call(
        reduce_kernel,
        out_shape=(sds((NS, T, GC), BF), sds((8, 128, 256), BF), sds((SMALL, 256), F32)),
        in_specs=[VM, VM, VM],
        out_specs=(VM, VM, VM),
        scratch_shapes=[
            v((NS, 128, GC), BF), v((NS, 512, 256), BF), v((NS, SMALL, 128), F32),
            v((NS, 128, GC), BF), v((NS, 512, 256), BF), v((NS, SMALL, 128), F32),
            v((NS, 128, GC), BF), v((3, 512, 256), BF), v((3, SMALL, 128), F32),
            v((8, 128), BF), v((512, 256), BF), v((SMALL, 128), F32),
            v((3, 128, GC), BF), v((3, 128, 256), BF), v((3, 16, 128), F32),
            v((128, GC), BF), v((128, 256), BF), v((16, 128), F32),
            v((3, 32, GC), BF), v((3, 32, 256), BF),
            v((NS, 128, GC), BF), v((NS, 128, 256), BF), v((3, 16, 128), F32), v((SMALL, 128), F32),
            DMA((48,)), DMA((48,)), DMA((3,)),
        ],
        compiler_params=pltpu.CompilerParams(collective_id=4, has_side_effects=True, vmem_limit_bytes=48 << 20),
        cost_estimate=pl.CostEstimate(flops=0, bytes_accessed=150 << 20, transcendentals=0),
        name="reduce_dense",
    )(a, b, g)


def member_rank(ids):
    e = lax.broadcasted_iota(jnp.int32, (NE, T), 0)
    m = jnp.zeros((NE, T), F32)
    for k in range(TOPK):
        m = jnp.where(ids[k : k + 1, :] == e, 1.0, m)
    before = (lax.broadcasted_iota(jnp.int32, (T, T), 0) < lax.broadcasted_iota(jnp.int32, (T, T), 1)).astype(F32)
    rank = nn(m.astype(BF), before.astype(BF))
    return jnp.where(m > 0.5, rank, -1.0)


def onehot(rank_row, weight_row=None):
    c = lax.broadcasted_iota(jnp.int32, (CAP, T), 0).astype(F32)
    hit = c == rank_row
    return jnp.where(hit, 1.0 if weight_row is None else weight_row, 0.0)


def pack_cot_kernel(ids, cot, rank, out):
    r = member_rank(ids[...])
    rank[...] = r
    rows = cot[...]
    for q in range(NE // 4):
        p = jnp.concatenate([onehot(r[e : e + 1, :]) for e in range(4 * q, 4 * q + 4)], axis=0)
        out[q * 4 * CAP : (q + 1) * 4 * CAP, :] = nn(p.astype(BF), rows).astype(BF)


def rotate(v, cos, sin):
    lane = lax.broadcasted_iota(jnp.int32, v.shape, 1)
    partner = jnp.where(lax.rem(lane, 64) < 32, pltpu.roll(v, 96, 1), pltpu.roll(v, 32, 1))
    return v * cos + partner * sin


def allowed_block(seg_col, seg_row, qb, kb):
    same = seg_col[kb * T : (kb + 1) * T, :] == seg_row[:, qb * T : (qb + 1) * T]
    if qb == kb:
        same = same & (
            lax.broadcasted_iota(jnp.int32, (T, T), 0) <= lax.broadcasted_iota(jnp.int32, (T, T), 1)
        )
    m = same.astype(F32)
    return jnp.concatenate([m, m], axis=1) > 0.5


def attend_kernel(x, w, gain, cos, sin, seg_col, seg_row, att, attt, hid, q8, k, v, logt):
    wall = w[...].reshape(D, GC)
    for b in range(NS):
        xb = x[b].astype(F32)
        scale = lax.rsqrt(jnp.mean(xb * xb, axis=-1, keepdims=True) + EPS)
        h = (xb * scale * gain[...]).astype(BF)
        hid[b] = h
        qkv = nn(h, wall)
        rows = slice(b * T, (b + 1) * T)
        c, s = cos[rows, :], sin[rows, :]
        q0 = rotate(qkv[:, 0:128], c, s)
        q1 = rotate(qkv[:, 128:256], c, s)
        q8[rows, 0:128] = (q0 * HD**-0.5).astype(BF)
        q8[rows, 128:256] = (q1 * HD**-0.5).astype(BF)
        k[rows, :] = rotate(qkv[:, 256:384], c, s).astype(BF)
        v[rows, :] = qkv[:, 384:512].astype(BF)
    vt = [v[b * T : (b + 1) * T, :].astype(F32).T.astype(BF) for b in range(NS)]
    for qb in range(NS):
        rows = slice(qb * T, (qb + 1) * T)
        masks = [allowed_block(seg_col[...], seg_row[...], qb, kb) for kb in range(qb + 1)]
        parts = []
        for j in range(2):
            qs = jnp.concatenate([q8[rows, 128 * j : 128 * j + 64], q8[rows, 128 * j + 64 : 128 * j + 128]], axis=0)
            total = jnp.zeros((1, 2 * T), F32)
            ot = jnp.zeros((HD, 2 * T), F32)
            for kb in range(qb + 1):
                st = nt(k[kb * T : (kb + 1) * T, 64 * j : 64 * j + 64], qs)
                e = jnp.where(masks[kb], jnp.exp(st), 0.0)
                total = total + jnp.sum(e, axis=0, keepdims=True)
                ot = ot + nn(vt[kb][64 * j : 64 * j + 64, :], e.astype(BF))
            logt[qb * 2 + j : qb * 2 + j + 1, :] = jnp.log(total)
            ot = ot / total
            parts += [ot[:, :T], ot[:, T:]]
        at = jnp.concatenate(parts, axis=0)
        attt[qb] = at.astype(BF)
        att[qb] = at.T.astype(BF)


def attend_back_kernel(da, attt, hid, q8, k, v, logt, cos, sin, seg_col, seg_row, dqkv, gw, dk, dv):
    dk[...] = jnp.zeros_like(dk)
    dv[...] = jnp.zeros_like(dv)
    kt = [k[b * T : (b + 1) * T, :].astype(F32).T.astype(BF) for b in range(NS)]
    for qb in range(NS):
        rows = slice(qb * T, (qb + 1) * T)
        masks = [allowed_block(seg_col[...], seg_row[...], qb, kb) for kb in range(qb + 1)]
        dab = da[qb]
        prod = dab.astype(F32).T * attt[qb].astype(F32)
        parts = []
        for j in range(2):
            qs = jnp.concatenate([q8[rows, 128 * j : 128 * j + 64], q8[rows, 128 * j + 64 : 128 * j + 128]], axis=0)
            do = jnp.concatenate([dab[:, 128 * j : 128 * j + 64], dab[:, 128 * j + 64 : 128 * j + 128]], axis=0)
            delta = jnp.concatenate(
                [
                    jnp.sum(prod[128 * j : 128 * j + 64, :], axis=0, keepdims=True),
                    jnp.sum(prod[128 * j + 64 : 128 * j + 128, :], axis=0, keepdims=True),
                ],
                axis=1,
            )
            lt = logt[qb * 2 + j : qb * 2 + j + 1, :]
            dqt = jnp.zeros((HD, 2 * T), F32)
            for kb in range(qb + 1):
                keys = slice(kb * T, (kb + 1) * T)
                cols = slice(64 * j, 64 * j + 64)
                p = jnp.where(masks[kb], jnp.exp(nt(k[keys, cols], qs) - lt), 0.0)
                dv[keys, cols] += nn(p.astype(BF), do)
                dp = nt(v[keys, cols], do)
                ds = (p * (dp - delta)).astype(BF)
                dk[keys, cols] += nn(ds, qs)
                dqt = dqt + nn(kt[kb][cols, :], ds)
            dqt = dqt * HD**-0.5
            parts += [dqt[:, :T], dqt[:, T:]]
        dq = jnp.concatenate(parts, axis=0).T
        c, s = cos[rows, :], -sin[rows, :]
        dqkv[qb, :, 0:128] = rotate(dq[:, 0:128], c, s).astype(BF)
        dqkv[qb, :, 128:256] = rotate(dq[:, 128:256], c, s).astype(BF)
    for b in range(NS):
        rows = slice(b * T, (b + 1) * T)
        dqkv[b, :, 256:384] = rotate(dk[rows, :], cos[rows, :], -sin[rows, :]).astype(BF)
        dqkv[b, :, 384:512] = dv[rows, :].astype(BF)
    for r in range(NS):
        acc = jnp.zeros((T, GC), F32)
        for b in range(NS):
            acc = acc + tn(hid[b, :, r * T : (r + 1) * T], dqkv[b])
        gw[r] = acc.astype(BF)


def middle_kernel(att, x, wo, gain, router, rank, resid, hid, pgate, gates, out):
    cols = []
    for s in range(NS):
        acc = x[:, s * 256 : (s + 1) * 256].astype(F32)
        for g in range(NS):
            acc = acc + nn(att[g], wo[s, g * 256 : (g + 1) * 256, :])
        cols.append(acc)
    r = jnp.concatenate(cols, axis=1)
    resid[...] = r
    scale = lax.rsqrt(jnp.mean(r * r, axis=-1, keepdims=True) + EPS)
    h = (r * scale * gain[...]).astype(BF)
    hid[...] = h
    logits = nt(router[...].astype(BF), h)
    rk = rank[...]
    ex = jnp.where(rk >= 0.0, jnp.exp(logits), 0.0)
    gt = ex / jnp.sum(ex, axis=0, keepdims=True)
    gates[...] = gt
    for q in range(NE // 4):
        es = range(4 * q, 4 * q + 4)
        rows = slice(q * 4 * CAP, (q + 1) * 4 * CAP)
        p = jnp.concatenate([onehot(rk[e : e + 1, :]) for e in es], axis=0)
        out[rows, :] = nn(p.astype(BF), h).astype(BF)
        w = jnp.concatenate([onehot(rk[e : e + 1, :], gt[e : e + 1, :]) for e in es], axis=0)
        pgate[rows, :] = w.astype(BF)


def expert_kernel(h, cot, wg, wu, wd, drow, mid, dgp, dup, dg):
    hb = h[...]
    gp = nn(hb, wg[...])
    up = nn(hb, wu[...])
    dm = nt(cot[:, 0:256], wd[0])
    for s in range(1, NS):
        dm = dm + nt(cot[:, s * 256 : (s + 1) * 256], wd[s])
    sig = jax.nn.sigmoid(gp)
    act = gp * sig
    m = (act * up).astype(BF)
    mid[...] = m
    dg[...] = jnp.sum(dm * m.astype(F32), axis=1, keepdims=True)
    a = (dm * up * sig * (1.0 + gp * (1.0 - sig))).astype(BF)
    b = (dm * act).astype(BF)
    dgp[...] = a
    dup[...] = b
    drow[...] = (nt(a, wg[...]) + nt(b, wu[...])).astype(BF)


def experts(h, cot, wg, wu, wd):
    rows = 288
    full = lambda *sh: pl.BlockSpec(sh, lambda n: (0,) * len(sh), pipeline_mode=pl.Buffered(1))
    tile = lambda c: pl.BlockSpec((rows, c), lambda n: (n, 0))
    return pl.pallas_call(
        expert_kernel,
        grid=(SLOTS // rows,),
        out_shape=(sds((SLOTS, D), BF), sds((SLOTS, FF), BF), sds((SLOTS, FF), BF), sds((SLOTS, FF), BF), sds((SLOTS, 1), F32)),
        in_specs=[tile(D), tile(D), full(D, FF), full(D, FF), full(NS, FF, 256)],
        out_specs=(tile(D), tile(FF), tile(FF), tile(FF), tile(1)),
        compiler_params=pltpu.CompilerParams(vmem_limit_bytes=48 << 20),
        cost_estimate=pl.CostEstimate(flops=12 << 30, bytes_accessed=24 << 20, transcendentals=0),
        name="experts",
    )(h, cot, wg, wu, wd)


def middle_back_kernel(back, dgs, pgate, rank, gates, router, resid, gain, cot, wo, att, hid, dres, dat, gwo, small):
    rk, gt = rank[...], gates[...]
    dh = jnp.zeros((T, D), F32)
    rowsd = []
    for q in range(NE // 4):
        rows = slice(q * 4 * CAP, (q + 1) * 4 * CAP)
        dh = dh + tn(pgate[rows, :], back[rows, :])
        for e in range(4 * q, 4 * q + 4):
            rowsd.append(jnp.sum(onehot(rk[e : e + 1, :], dgs[:, e : e + 1]), axis=0, keepdims=True))
    dgate = jnp.concatenate(rowsd, axis=0)
    dch = gt * (dgate - jnp.sum(gt * dgate, axis=0, keepdims=True))
    dl = dch.astype(BF)
    small[0:NE, :] = nn(dl, hid[...])
    dh = dh + tn(dl, router[...].astype(BF))
    r = resid[...]
    scale = lax.rsqrt(jnp.mean(r * r, axis=-1, keepdims=True) + EPS)
    normed = r * scale
    small[NE : NE + 1, :] = jnp.sum(dh * normed, axis=0, keepdims=True)
    small[NE + 1 :, :] = jnp.zeros((SMALL - NE - 1, D), F32)
    m = dh * gain[...]
    dr = cot[...].astype(F32) + scale * (m - normed * jnp.mean(m * normed, axis=-1, keepdims=True))
    dres[...] = dr
    da = dr.astype(BF)
    for g in range(NS):
        acc = jnp.zeros((T, 256), F32)
        for s in range(NS):
            acc = acc + nt(da[:, s * 256 : (s + 1) * 256], wo[s, g * 256 : (g + 1) * 256, :])
        dat[g] = acc.astype(BF)
    for s in range(NS):
        for g in range(NS):
            gwo[s, g * 256 : (g + 1) * 256, :] = tn(att[g], da[:, s * 256 : (s + 1) * 256]).astype(BF)


def first_back_kernel(dqkv, wq, wk, wv, x, gain, dres, dtok, gnorm):
    dh = jnp.zeros((T, D), F32)
    for g in range(NS):
        dh = dh + nt(dqkv[g, :, 0:256], wq[:, g * 256 : (g + 1) * 256])
        dh = dh + nt(dqkv[g, :, 256:384], wk[:, g * 128 : (g + 1) * 128])
        dh = dh + nt(dqkv[g, :, 384:512], wv[:, g * 128 : (g + 1) * 128])
    xf = x[...].astype(F32)
    scale = lax.rsqrt(jnp.mean(xf * xf, axis=-1, keepdims=True) + EPS)
    normed = xf * scale
    gnorm[...] = jnp.broadcast_to(jnp.sum(dh * normed, axis=0, keepdims=True), (8, D))
    n = dh * gain[...]
    dtok[...] = (dres[...] + scale * (n - normed * jnp.mean(n * normed, axis=-1, keepdims=True))).astype(BF)


def per_device(
    tokens, segments, expert_ids, attn_norm, query_weight, key_matrix, value_matrix, output_weight,
    ffn_norm, router_weight, gate_weight, up_weight, down_weight, cotangent,
):
    a2a = lambda v: lax.all_to_all(v, "expert", split_axis=0, concat_axis=0, tiled=True)
    gather = lambda v, axis: lax.all_gather(v, "shard", axis=axis, tiled=True)
    stack = lambda v: lax.all_gather(v, "shard", axis=0, tiled=False)

    rank, cot_rows = plain(
        pack_cot_kernel, (sds((NE, T), F32), sds((SLOTS, D), BF)), expert_ids.T, cotangent,
        name="pack_cot", flops=2 << 30, moved=6 << 20,
    )
    cot_recv = a2a(cot_rows.reshape(NE, CAP, D)).reshape(SLOTS, D)

    small = jnp.concatenate(
        [
            router_weight.T.astype(F32),
            attn_norm.astype(F32)[None],
            ffn_norm.astype(F32)[None],
            segments.astype(F32),
            jnp.zeros((5, T), F32),
        ],
        axis=0,
    )
    x_all, w_group, small_all = gather_front(tokens, query_weight, key_matrix, value_matrix, small)
    small_full = small_all.transpose(1, 0, 2).reshape(40, D)
    router, gain_one, gain_two, seg_row = small_full[:NE], small_full[32:33], small_full[33:34], small_full[34:35]
    seg_col = seg_row.reshape(D, 1)

    wo = stack(output_weight)
    wg = gather(gate_weight[0], 0)
    wu = gather(up_weight[0], 0)
    wd = stack(down_weight[0])
    wq = gather(query_weight, 0)
    wk = gather(key_matrix, 0)
    wv = gather(value_matrix, 0)

    inverse = BASE ** (-jnp.arange(HD // 2, dtype=F32) * 2.0 / HD)
    angles = jnp.arange(D, dtype=F32)[:, None] * inverse[None, :]
    co, si = jnp.cos(angles), jnp.sin(angles)
    cos = jnp.concatenate([co, co, co, co], axis=1)
    sin = jnp.concatenate([-si, si, -si, si], axis=1)

    att, attt, hid_one, q8, k, v, logt = plain(
        attend_kernel,
        (
            sds((NS, T, 256), BF), sds((NS, 256, T), BF), sds((NS, T, D), BF), sds((D, 256), BF),
            sds((D, 128), BF), sds((D, 128), BF), sds((8, 512), F32),
        ),
        x_all, w_group, gain_one, cos, sin, seg_col, seg_row,
        name="attend", flops=2 << 30, moved=10 << 20,
    )
    att_rows = swap(att, 1)
    resid, hid_two, pgate, gates, send = plain(
        middle_kernel,
        (sds((T, D), F32), sds((T, D), BF), sds((SLOTS, T), BF), sds((NE, T), F32), sds((SLOTS, D), BF)),
        att_rows, tokens, wo, gain_two, router, rank,
        name="middle", flops=2 << 30, moved=10 << 20,
    )
    recv = a2a(send.reshape(NE, CAP, D)).reshape(SLOTS, D)
    hit = rank[:, None, :] == jnp.arange(CAP, dtype=F32)[None, :, None]
    gate_slots = jnp.sum(jnp.where(hit, gates[:, None, :], 0.0), axis=2)
    gate_recv = a2a(gate_slots).reshape(SLOTS, 1)

    drow, mid, dgp, dup, dg = experts(recv, cot_recv, wg, wu, wd)
    back = a2a(drow.reshape(NE, CAP, D)).reshape(SLOTS, D)
    dgs = a2a(dg.reshape(NE, CAP)).T

    wd_rows = wd.transpose(1, 0, 2).reshape(FF, D)
    out_rows = jnp.dot(mid, wd_rows, preferred_element_type=F32).astype(BF)
    out_back = a2a(out_rows.reshape(NE, CAP, D)).reshape(SLOTS, D)
    scaled = lambda u: (u.astype(F32) * gate_recv).astype(BF)
    grad_down = jnp.einsum("nf,nd->fd", mid, scaled(cot_recv), preferred_element_type=F32)
    grad_gate = jnp.einsum("nd,nf->df", recv, scaled(dgp), preferred_element_type=F32)
    grad_up = jnp.einsum("nd,nf->df", recv, scaled(dup), preferred_element_type=F32)
    scatter = lambda u, d: lax.psum_scatter(u[None].astype(BF), "shard", scatter_dimension=d, tiled=True).astype(F32)
    d_gate, d_up, d_down = scatter(grad_gate, 1), scatter(grad_up, 1), scatter(grad_down, 2)

    combined = jnp.einsum("nt,nd->td", pgate, out_back, preferred_element_type=F32)
    output = (resid + combined).astype(BF)

    dres, dat, gwo, small_grad = plain(
        middle_back_kernel,
        (sds((T, D), F32), sds((NS, T, 256), BF), sds((NS, D, 256), BF), sds((SMALL, D), F32)),
        back, dgs, pgate, rank, gates, router, resid, gain_two, cotangent, wo, att_rows, hid_two,
        name="middle_back", flops=4 << 30, moved=14 << 20,
    )
    dat_seq = swap(dat, 2)
    dqkv, gw = plain(
        attend_back_kernel,
        (sds((NS, T, GC), BF), sds((NS, T, GC), BF)),
        dat_seq, attt, hid_one, q8, k, v, logt, cos, sin, seg_col, seg_row,
        name="attend_back", flops=4 << 30, moved=10 << 20,
        scratch_shapes=[pltpu.VMEM((D, 128), F32), pltpu.VMEM((D, 128), F32)],
    )
    dqkv_rows = swap(dqkv, 3)
    d_tokens, gnorm = plain(
        first_back_kernel,
        (sds((T, D), BF), sds((8, D), F32)),
        dqkv_rows, wq, wk, wv, tokens, gain_one, dres,
        name="first_back", flops=1 << 30, moved=8 << 20,
    )
    small_sum = jnp.concatenate([small_grad[: NE + 1], gnorm[:1], small_grad[NE + 2 :]], axis=0)
    ga, gb, gs = reduce_dense(gw, gwo, small_sum.reshape(SMALL, NS, T).transpose(1, 0, 2))
    ga, gb = ga.astype(F32), gb.astype(F32)
    d_query = ga[:, :, 0:256].transpose(1, 0, 2).reshape(T, D)
    d_key = ga[:, :, 256:384].transpose(1, 0, 2).reshape(T, 512)
    d_value = ga[:, :, 384:512].transpose(1, 0, 2).reshape(T, 512)
    d_output_weight = gb.reshape(D, 256)
    d_router, d_ffn_norm, d_attn_norm = gs[:NE].T, gs[NE], gs[NE + 1]
    return (
        output, d_tokens, d_attn_norm, d_query, d_key, d_value, d_output_weight, d_ffn_norm, d_router,
        d_gate, d_up, d_down,
    )


def solution(mesh):
    rows = P(("expert", "shard"), None)
    return jax.shard_map(
        per_device,
        mesh=mesh,
        in_specs=(
            rows, P("expert", "shard"), rows, P("shard"), P("shard", None), P("shard", None), P("shard", None),
            P(None, "shard"), P("shard"), P("shard", None), P("expert", "shard", None), P("expert", "shard", None),
            P("expert", None, "shard"), rows,
        ),
        out_specs=(
            rows, rows, P("shard"), P("shard", None), P("shard", None), P("shard", None), P(None, "shard"),
            P("shard"), P("shard", None), P("expert", "shard", None), P("expert", "shard", None),
            P("expert", None, "shard"),
        ),
        check_vma=False,
    )
```

time: 971 us -> 545 us (0.56)
  waiting for transfers between devices: 424 us -> 168 us
  Pallas kernels: 0 us -> 221 us
  blocking collectives: 162 us -> 32.4 us
  matrix products: 139 us -> 30.6 us
  local copies, waits for them, and re-layouts: 118 us -> 24.3 us
  other arithmetic: 60.8 us -> 15.7 us
    pallas_call x0 -> x12, Pallas kernels: none -> 221 us  [the longest x1 60.2 us: reduce_dense(): pl.pallas_call(reduce_kernel, out_shape=(sds((NS, T, GC), BF), sds((8, 12...]
    reduce_scatter x10 -> x3, waiting for transfers between devices: 191 us -> 0.01 us  [per_device(): lax.psum_scatter(u[None].astype(BF), 'shard', scatter_dimension=d, tiled=...]
    psum x1 -> x0, blocking collectives: 123 us -> none  [per_device(): lax.psum(partial_sums[0].astype(jnp.bfloat16), 'expert').astype(jnp.float32)]
    dot_general x29 -> x5, matrix products: 125 us -> 30.6 us  [the longest x1 6.89 us: per_device(): jnp.einsum('nd,nf->df', recv, scaled(dgp), preferred_element_type=F32)]
    all_gather x9 -> x7, waiting for transfers between devices: 148 us -> 56.5 us  [the longest x5 56.5 us: per_device(): gather = lambda v, axis: lax.all_gather(v, 'shard', axis=axis, tiled=True)]
    gather x2 -> x0, local copies, waits for them, and re-layouts: 81.6 us -> none  [the longest x1 40.8 us: per_device(): returned[flat_ids, slot_pos].astype(single_float)]
    all_to_all x0 -> x2, blocking collectives: none -> 32.4 us  [per_device(): lax.all_to_all(v, 'expert', split_axis=0, concat_axis=0, tiled=True)]
    all_gather x4 -> x0, blocking collectives: 32.1 us -> none  [the longest x1 10.2 us: gather_weights(): lax.all_gather(weights[6], 'shard', axis=0, tiled=True)]
  transfers between devices with their start and end apart: 24 -> 14, of which waited for: 20 -> 6; matrix products, arithmetic and copies ran while one was open for 21% -> 10% of each run, Pallas kernels for 0% -> 37%
where the time goes in v1:
time: 545 us; the launch traced here: 535 us
  Pallas kernels  221 us (41%)
  waiting for transfers between devices  168 us (31%)
  blocking collectives  32.4 us (6%)
  matrix products  30.6 us (6%)
  starting transfers between devices  28.4 us (5%)
  local copies, waits for them, and re-layouts  24.3 us (4%)
  other arithmetic  15.7 us (3%)
  between operations  14.7 us (3%)
    all_to_all x4, waiting for transfers between devices, per_device(): lax.all_to_all(v, 'expert', split_axis=0, concat_axis=0, tiled=True)  107 us
    pallas_call x1, Pallas kernels, reduce_dense(): pl.pallas_call(reduce_kernel, out_shape=(sds((NS, T, GC), BF), sds((8, 12...  60.2 us
    all_gather x5, waiting for transfers between devices, per_device(): gather = lambda v, axis: lax.all_gather(v, 'shard', axis=axis, tiled=True)  56.5 us
    pallas_call x6, Pallas kernels, plain(): pl.pallas_call(kernel, out_shape=outs, in_specs=[VM] * len(args), out_spe...  51.7 us
    pallas_call x3, Pallas kernels, swap(): pl.pallas_call(swap_kernel, out_shape=sds(x.shape, x.dtype), in_specs=[AN...  47 us
    pallas_call x1, Pallas kernels, gather_front(): pl.pallas_call(gather_front_kernel, out_shape=(sds((NS, T, D), BF), sds((...  44.3 us
    all_to_all x2, blocking collectives, per_device(): lax.all_to_all(v, 'expert', split_axis=0, concat_axis=0, tiled=True)  32.4 us
    all_to_all x4, starting transfers between devices, per_device(): lax.all_to_all(v, 'expert', split_axis=0, concat_axis=0, tiled=True)  28 us
  transfers between devices with their start and end apart: 14, of which 6 were waited for; matrix products, arithmetic and copies ran while one was open for 10% of the time, Pallas kernels for 37%

profile of v1, /device:TPU:1, one launch (start us, length us, event | category | flops | bytes accessed | tf_op | source)
XLA Modules:
  0.0 534.9 jit_solution(4014676201725927645)
XLA Ops:
  7.2 0.7 all-gather.19.cloned.1.call-update
  7.9 0.7 broadcast_in_dim.42
  8.6 0.7 broadcast_in_dim.43
  9.2 0.7 convert_element_type.68
  9.9 0.7 convert_bitcast_fusion
  10.6 1.2 concatenate.12.small
  11.9 44.3 %gather_front.1 = (bf16[4,256,1024]{2,1,0:T(8,128)(2,1)}, bf16[4,256,512]{2,1,0:T(8,128)(2,1)}, f32[4,40,256]{2,1,0:T(8,128)}) custom-call(bf16[256,1024]{1,0:T(8,128)(2,1)} %x.5, bf16[256,1024]{1,0:T(8,128)(2,1)} %wq.1, bf16[256,512]{1,0:T(8,128)(2,1)} %wk.1, bf16[256,512]{1,0:T(8,128)(2,1)} %wv.1, f32[40,256]{1,0:T(8,128)} %concatenate.12.small), custom_call_target="tpu_custom_call" | custom-call | bytes 94371840 | tf_op jit(solution)/shard_map/gather_front/pallas_call | solution.py:121
  56.2 1.5 fusion.16
  57.7 1.0 copy.52.seg_col
  58.7 2.0 fusion.15
  60.7 1.8 pad_maximum_fusion
  62.5 10.3 %attend.1 = (bf16[4,256,256]{2,1,0:T(8,128)(2,1)}, bf16[4,256,256]{2,1,0:T(8,128)(2,1)}, bf16[4,256,1024]{2,1,0:T(8,128)(2,1)}, bf16[1024,256]{1,0:T(8,128)(2,1)...) custom-call(bf16[4,256,1024]{2,1,0:T(8,128)(2,1)} %get-tuple-element.45.x, ...), custom_call_target="tpu_custom_call" | custom-call | flops 2147483648 | bytes 10485760 | tf_op jit(solution)/shard_map/attend/pallas_call | solution.py:50
  72.9 8.4 %swap1.1.att = bf16[4,256,256]{2,1,0:T(8,128)(2,1)} custom-call(bf16[4,256,256]{2,1,0:T(8,128)(2,1)} %get-tuple-element.48.x), custom_call_target="tpu_custom_call" | custom-call | bytes 31457280 | tf_op jit(solution)/shard_map/swap1/pallas_call | solution.py:153
  81.3 0.7 copy.67
  82.0 4.7 pack_cot.1
  86.7 6.8 %middle.1 = (f32[256,1024]{1,0:T(8,128)}, bf16[256,1024]{1,0:T(8,128)(2,1)}, bf16[2304,256]{1,0:T(8,128)(2,1)}, f32[32,256]{1,0:T(8,128)}, bf16[2304,1024]{1,0:T(8,128)(2,1)}) custom-call(bf16[4,256,256]{2,1,0:T(8,128)(2,1)} %swap1.1.att, bf16[256,1024]{1,0:T(8,128)(2,1)} %x.5, bf16[4,1024,256]{2,1,0:T(8,128)(2,1)} %bitcast.100, f32[1,1024]{1,0:T(1,128)} %bitcast.94, ...), custom_call_target="tpu_custom_call" | custom-call | flops 2147483648 | bytes 10485760 | tf_op jit(solution)/shard_map/middle/pallas_call | solution.py:50
  93.5 1.4 select_reduce_fusion
  94.9 18.6 %all_to_all.41 = f32[32,1,72]{2,1,0:T(1,128)S(1)} all-to-all(f32[32,1,72]{2,1,0:T(1,128)S(1)} %bitcast.86), channel_id=1, replica_groups=mesh['expert'=32,'shard'=4] {'expert'}, dimensions={0} | all-to-all | bytes 18432 | tf_op jit(solution)/shard_map/all_to_all | solution.py:540
  113.5 5.1 all-to-all-start.1
  118.7 0.7 all-gather.11.cloned.1.call-update
  119.4 55.1 %all-to-all-done.1 = bf16[32,72,1024]{2,1,0:T(8,128)(2,1)} async-done(((bf16[32,72,1024]{2,1,0:T(8,128)(2,1)}), bf16[32,72,1024]{2,1,0:T(8,128)(2,1)}, u32[]{:S(2)}, u32[]{:S(2)}) %all-to-all-start.1) | async-done | bytes 4718624 | tf_op jit(solution)/shard_map/all_to_all | solution.py:540
  174.5 8.8 %all-to-all-start = ((bf16[32,72,1024]{2,1,0:T(8,128)(2,1)}), bf16[32,72,1024]{2,1,0:T(8,128)(2,1)}, u32[]{:S(2)}, u32[]{:S(2)}) async-start(bf16[32,72,1024]{2,1,0:T(8,128)(2,1)} %bitcast.75), calls=%async_computation | async-start | bytes 9437184 | tf_op jit(solution)/shard_map/all_to_all | solution.py:540
  183.3 0.7 all-gather.21.cloned.1.call-update
  185.1 0.7 reduce.4
  186.0 22.9 %all-gather.21.cloned.1.call-done = bf16[1,1024,512]{2,1,0:T(8,128)(2,1)} async-done(((bf16[1,256,512]{2,1,0:T(8,128)(2,1)}), bf16[1,1024,512]{2,1,0:T(8,128)(2,1)}) %all-gather.21.cloned.1.call-update) | async-done | bytes 1048592 | tf_op jit(solution)/shard_map/all_gather | solution.py:541
  208.9 25.8 %all-gather.23.cloned.1.call-done = bf16[1,1024,512]{2,1,0:T(8,128)(2,1)} async-done(((bf16[1,256,512]{2,1,0:T(8,128)(2,1)}), bf16[1,1024,512]{2,1,0:T(8,128)(2,1)}) %all-gather.23.cloned.1.call-update) | async-done | bytes 1048592 | tf_op jit(solution)/shard_map/all_gather | solution.py:541
  234.7 4.4 all-to-all-done
  239.1 1.2 copy-done.1
  240.3 1.2 copy-done.4
  241.6 1.2 copy-done.5
  242.8 17.8 %experts.1 = (bf16[2304,1024]{1,0:T(8,128)(2,1)}, bf16[2304,512]{1,0:T(8,128)(2,1)}, bf16[2304,512]{1,0:T(8,128)(2,1)}, bf16[2304,512]{1,0:T(8,128)(2,1)}, f32[2304,1]{1,0:T(8,128)S(1)}) custom-call(bf16[2304,1024]{1,0:T(8,128)(2,1)} %bitcast.11.h, bf16[2304,1024]{1,0:T(8,128)(2,1)} %bitcast.13.cot, bf16[1024,512]{1,0:T(8,128)(2,1)S(1)} %bitcast.71, ...), custom_call_target="tpu_custom_call" | custom-call | flops 12884901888 | bytes 25165824 | tf_op jit(solution)/shard_map/experts/pallas_call | solution.py:477
  260.6 6.8 %fusion.11 = bf16[1,1024,512]{2,1,0:T(8,128)(2,1)} fusion(bf16[2304,1024]{1,0:T(8,128)(2,1)} %bitcast.11.h, bf16[2304,512]{1,0:T(8,128)(2,1)} %get-tuple-element.77, f32[2304]{0:T(1024)S(1)} %mul.85), kind=kOutput, calls=%fused_computation.17 | convolution fusion | flops 2419982336 | bytes 8135680 | tf_op jit(solution)/shard_map/nd,nf->df/dot_general | solution.py:610
  267.5 6.9 %fusion.10 = bf16[1,1024,512]{2,1,0:T(8,128)(2,1)} fusion(bf16[2304,1024]{1,0:T(8,128)(2,1)} %bitcast.11.h, bf16[2304,512]{1,0:T(8,128)(2,1)} %get-tuple-element.76, f32[2304]{0:T(1024)S(1)} %mul.85), kind=kOutput, calls=%fused_computation.16 | convolution fusion | flops 2419982336 | bytes 8135680 | tf_op jit(solution)/shard_map/nd,nf->df/dot_general | solution.py:609
  274.4 6.3 %fusion.9 = bf16[1,512,1024]{2,1,0:T(8,128)(2,1)} fusion(bf16[2304,512]{1,0:T(8,128)(2,1)S(1)} %copy-done.11, bf16[2304,1024]{1,0:T(8,128)(2,1)} %bitcast.13.cot, f32[2304]{0:T(1024)S(1)} %mul.85), kind=kOutput, calls=%fused_computation.15 | convolution fusion | flops 2423521280 | bytes 8135680 | tf_op jit(solution)/shard_map/nf,nd->fd/dot_general | solution.py:608
  281.3 13.8 %all_to_all.42 = f32[32,1,72]{2,1,0:T(1,128)S(1)} all-to-all(f32[32,1,72]{2,1,0:T(1,128)S(1)} %bitcast.87), channel_id=1, replica_groups=mesh['expert'=32,'shard'=4] {'expert'}, dimensions={0} | all-to-all | bytes 18432 | tf_op jit(solution)/shard_map/all_to_all | solution.py:540
  295.1 5.2 all-to-all-start.3
  300.3 0.7 all-gather.15.cloned.1.call-update
  301.1 0.7 all-gather.17.cloned.1.call-update
  302.9 6.0 %convolution_convert_fusion = bf16[2304,1024]{1,0:T(8,128)(2,1)} fusion(bf16[2304,512]{1,0:T(8,128)(2,1)} %get-tuple-element.54, bf16[512,1024]{0,1:T(8,128)(2,1)S(1)} %bitcast.80), kind=kOutput, calls=%fused_computation.1 | convolution fusion | flops 2418278400 | bytes 8126464 | tf_op jit(solution)/shard_map/dot_general | solution.py:605
  309.0 47.2 %all-to-all-done.3 = bf16[32,72,1024]{2,1,0:T(8,128)(2,1)} async-done(((bf16[32,72,1024]{2,1,0:T(8,128)(2,1)}), bf16[32,72,1024]{2,1,0:T(8,128)(2,1)}, u32[]{:S(2)}, u32[]{:S(2)}) %all-to-all-start.3) | async-done | bytes 4718624 | tf_op jit(solution)/shard_map/all_to_all | solution.py:540
  356.1 8.9 %all-to-all-start.2 = ((bf16[32,72,1024]{2,1,0:T(8,128)(2,1)}), bf16[32,72,1024]{2,1,0:T(8,128)(2,1)}, u32[]{:S(2)}, u32[]{:S(2)}) async-start(bf16[32,72,1024]{2,1,0:T(8,128)(2,1)} %bitcast.73), calls=%async_computation.2 | async-start | bytes 9437184 | tf_op jit(solution)/shard_map/all_to_all | solution.py:540
  365.1 0.7 copy.56
  365.8 1.8 convert_element_type.81
  367.6 1.8 convert_element_type.76
  369.4 1.8 convert_element_type.86
  371.2 9.6 %middle_back.1 = (f32[256,1024]{1,0:T(8,128)}, bf16[4,256,256]{2,1,0:T(8,128)(2,1)}, bf16[4,1024,256]{2,1,0:T(8,128)(2,1)}, f32[64,1024]{1,0:T(8,128)}) custom-call(bf16[2304,1024]{1,0:T(8,128)(2,1)} %bitcast.21.back, f32[72,32]{1,0:T(8,128)} %bitcast.88, bf16[2304,256]{1,0:T(8,128)(2,1)} %get-tuple-element.51.pgate, f32[32,256]{1,0:T(8,128)} %get-tuple-element.49.rank, ...), custom_call_target="tpu_custom_call" | custom-call | flops 4294967296 | bytes 14680064 | tf_op jit(solution)/shard_map/middle_back/pallas_call | solution.py:50
  380.8 0.9 slice.59
  381.7 0.9 slice.61
  382.6 13.5 %swap2.1.da = bf16[4,256,256]{2,1,0:T(8,128)(2,1)} custom-call(bf16[4,256,256]{2,1,0:T(8,128)(2,1)} %get-tuple-element.59.x), custom_call_target="tpu_custom_call" | custom-call | bytes 31457280 | tf_op jit(solution)/shard_map/swap2/pallas_call | solution.py:153
  396.1 14.2 %attend_back.1 = (bf16[4,256,512]{2,1,0:T(8,128)(2,1)}, bf16[4,256,512]{2,1,0:T(8,128)(2,1)}) custom-call(bf16[4,256,256]{2,1,0:T(8,128)(2,1)} %swap2.1.da, bf16[4,256,256]{2,1,0:T(8,128)(2,1)} %get-tuple-element.60.attt, bf16[4,256,1024]{2,1,0:T(8,128)(2,1)} %get-tuple-element.61.hid, bf16[1024,256]{1,0:T(8,128)(2,1)} %get-tuple-element.62.q8, ...), custom_call_target="tpu_custom_call" | custom-call | flops 4294967296 | bytes 10485760 | tf_op jit(solution)/shard_map/attend_back/pallas_call | solution.py:50
  410.4 25.1 %swap3.1.dqkv = bf16[4,256,512]{2,1,0:T(8,128)(2,1)} custom-call(bf16[4,256,512]{2,1,0:T(8,128)(2,1)} %get-tuple-element.66.x), custom_call_target="tpu_custom_call" | custom-call | bytes 31457280 | tf_op jit(solution)/shard_map/swap3/pallas_call | solution.py:153
  435.6 7.7 %all-gather.13.cloned.1.call-done.wq = bf16[1024,1024]{1,0:T(8,128)(2,1)} async-done(((bf16[256,1024]{1,0:T(8,128)(2,1)}), bf16[1024,1024]{1,0:T(8,128)(2,1)}) %all-gather.13.cloned.1.call-update) | async-done | bytes 2097168 | tf_op jit(solution)/shard_map/all_gather | solution.py:541
  443.2 5.9 %first_back.1 = (bf16[256,1024]{1,0:T(8,128)(2,1)}, f32[8,1024]{1,0:T(8,128)}) custom-call(bf16[4,256,512]{2,1,0:T(8,128)(2,1)} %swap3.1.dqkv, bf16[1024,1024]{1,0:T(8,128)(2,1)} %all-gather.13.cloned.1.call-done.wq, bf16[1024,512]{1,0:T(8,128)(2,1)} %all-gather.15.cloned.1.call-done.wk, bf16[1024,512]{1,0:T(8,128)(2,1)} %all-gather.17.cloned.1.call-done.wv, ...), custom_call_target="tpu_custom_call" | custom-call | flops 1073741824 | bytes 8388608 | tf_op jit(solution)/shard_map/first_back/pallas_call | solution.py:50
  449.2 0.8 slice.60
  450.0 60.2 %reduce_dense.1 = (bf16[4,256,512]{2,1,0:T(8,128)(2,1)S(1)}, bf16[8,128,256]{2,1,0:T(8,128)(2,1)S(1)}, f32[64,256]{1,0:T(8,128)S(1)}) custom-call(bf16[4,256,512]{2,1,0:T(8,128)(2,1)S(1)} %copy-done.3, bf16[4,1024,256]{2,1,0:T(8,128)(2,1)S(1)} %copy-done, f32[4,64,256]{2,1,0:T(8,128)S(1)} %bitcast.70), custom_call_target="tpu_custom_call" | custom-call | bytes 157286400 | tf_op jit(solution)/shard_map/reduce_dense/pallas_call | solution.py:279
  510.5 1.1 slice_bitcast_fusion
  511.6 2.5 copy.59
  514.2 2.5 copy.63
  516.7 0.9 slice_bitcast_fusion.1
  517.6 1.2 copy.60
  518.8 1.0 copy.64
  520.0 1.0 copy.65
  522.2 1.1 bitcast_convert_fusion
  523.3 4.5 fusion.12
  (58 shorter events, 4.9 us)
Async XLA Ops:
  7.2 79.5 %all-gather.19.cloned.1.call-start = ((), (), s32[]{:S(2)}) async-start(), calls=%async_computation.16 | async-start | bytes 2621440 | tf_op jit(solution)/shard_map/all_gather | solution.py:542
  57.7 4.9 copy-start.8
  62.5 18.8 %copy-start.6 = (f32[4,40,256]{2,1,0:T(8,128)S(1)}, f32[4,40,256]{2,1,0:T(8,128)}, u32[]{:S(2)}) copy-start(f32[4,40,256]{2,1,0:T(8,128)} %get-tuple-element.47) | copy-start | bytes 491524
  86.7 6.8 %copy-start.7 = (f32[32,256]{1,0:T(8,128)S(1)}, f32[32,256]{1,0:T(8,128)}, u32[]{:S(2)}) copy-start(f32[32,256]{1,0:T(8,128)} %get-tuple-element.49.rank) | copy-start | bytes 98308
  113.5 61.0 %all-to-all-start.1 = ((bf16[32,72,1024]{2,1,0:T(8,128)(2,1)}), bf16[32,72,1024]{2,1,0:T(8,128)(2,1)}, u32[]{:S(2)}, u32[]{:S(2)}) async-start(bf16[32,72,1024]{2,1,0:T(8,128)(2,1)} %bitcast.76), calls=%async_computation.1 | async-start | bytes 9437184 | tf_op jit(solution)/shard_map/all_to_all | solution.py:540
  118.6 67.3 %all-gather.11.cloned.1.call-start = ((), (), s32[]{:S(2)}) async-start(), calls=%async_computation.9 | async-start | bytes 1310720 | tf_op jit(solution)/shard_map/all_gather | solution.py:542
  174.5 64.6 %all-to-all-start = ((bf16[32,72,1024]{2,1,0:T(8,128)(2,1)}), bf16[32,72,1024]{2,1,0:T(8,128)(2,1)}, u32[]{:S(2)}, u32[]{:S(2)}) async-start(bf16[32,72,1024]{2,1,0:T(8,128)(2,1)} %bitcast.75), calls=%async_computation | async-start | bytes 9437184 | tf_op jit(solution)/shard_map/all_to_all | solution.py:540
  183.3 25.6 %all-gather.21.cloned.1.call-start = ((), (), s32[]{:S(2)}) async-start(), calls=%async_computation.17 | async-start | bytes 1310720 | tf_op jit(solution)/shard_map/all_gather | solution.py:541
  184.0 50.7 %all-gather.23.cloned.1.call-start = ((), (), s32[]{:S(2)}) async-start(), calls=%async_computation.18 | async-start | bytes 1310720 | tf_op jit(solution)/shard_map/all_gather | solution.py:541
  184.6 181.2 %reduce-scatter.6.cloned.1.call-start = ((), (), s32[]{:S(2)}) async-start(), calls=%async_computation.14 | async-start | bytes 1310720 | tf_op jit(solution)/shard_map/reduce_scatter | solution.py:611
  239.1 1.2 copy-start.1
  240.3 1.2 copy-start.4
  241.6 1.2 copy-start.5
  267.4 100.2 %reduce-scatter.4.cloned.1.call-start = ((), (), s32[]{:S(2)}) async-start(), calls=%async_computation.13 | async-start | bytes 1310720 | tf_op jit(solution)/shard_map/reduce_scatter | solution.py:611
  267.4 7.0 %copy-start.11 = (bf16[2304,512]{1,0:T(8,128)(2,1)S(1)}, bf16[2304,512]{1,0:T(8,128)(2,1)}, u32[]{:S(2)}) copy-start(bf16[2304,512]{1,0:T(8,128)(2,1)} %get-tuple-element.54) | copy-start | bytes 7077892
  274.4 95.0 %reduce-scatter.8.cloned.1.call-start = ((), (), s32[]{:S(2)}) async-start(), calls=%async_computation.15 | async-start | bytes 1310720 | tf_op jit(solution)/shard_map/reduce_scatter | solution.py:611
  295.1 7.3 %copy-start.2 = (bf16[4,512,256]{2,1,0:T(8,128)(2,1)S(1)}, bf16[4,512,256]{2,1,0:T(8,128)(2,1)}, u32[]{:S(2)}) copy-start(bf16[4,512,256]{2,1,0:T(8,128)(2,1)} %all-gather.11.cloned.1.call-done.wd) | copy-start | bytes 3145732
  295.1 61.1 %all-to-all-start.3 = ((bf16[32,72,1024]{2,1,0:T(8,128)(2,1)}), bf16[32,72,1024]{2,1,0:T(8,128)(2,1)}, u32[]{:S(2)}, u32[]{:S(2)}) async-start(bf16[32,72,1024]{2,1,0:T(8,128)(2,1)} %bitcast.74), calls=%async_computation.3 | async-start | bytes 9437184 | tf_op jit(solution)/shard_map/all_to_all | solution.py:540
  300.3 135.2 %all-gather.15.cloned.1.call-start = ((), (), s32[]{:S(2)}) async-start(), calls=%async_computation.11 | async-start | bytes 1310720 | tf_op jit(solution)/shard_map/all_gather | solution.py:541
  301.0 134.5 %all-gather.17.cloned.1.call-start = ((), (), s32[]{:S(2)}) async-start(), calls=%async_computation.12 | async-start | bytes 1310720 | tf_op jit(solution)/shard_map/all_gather | solution.py:541
  301.8 141.4 %all-gather.13.cloned.1.call-start = ((), (), s32[]{:S(2)}) async-start(), calls=%async_computation.10 | async-start | bytes 2621440 | tf_op jit(solution)/shard_map/all_gather | solution.py:541
  356.1 167.2 %all-to-all-start.2 = ((bf16[32,72,1024]{2,1,0:T(8,128)(2,1)}), bf16[32,72,1024]{2,1,0:T(8,128)(2,1)}, u32[]{:S(2)}, u32[]{:S(2)}) async-start(bf16[32,72,1024]{2,1,0:T(8,128)(2,1)} %bitcast.73), calls=%async_computation.2 | async-start | bytes 9437184 | tf_op jit(solution)/shard_map/all_to_all | solution.py:540
  443.2 6.8 %copy-start = (bf16[4,1024,256]{2,1,0:T(8,128)(2,1)S(1)}, bf16[4,1024,256]{2,1,0:T(8,128)(2,1)}, u32[]{:S(2)}) copy-start(bf16[4,1024,256]{2,1,0:T(8,128)(2,1)} %get-tuple-element.70.b) | copy-start | bytes 6291460
  443.2 6.8 %copy-start.3 = (bf16[4,256,512]{2,1,0:T(8,128)(2,1)S(1)}, bf16[4,256,512]{2,1,0:T(8,128)(2,1)}, u32[]{:S(2)}) copy-start(bf16[4,256,512]{2,1,0:T(8,128)(2,1)} %get-tuple-element.69.a) | copy-start | bytes 3145732
  518.8 4.5 copy-start.9
  520.0 3.3 copy-start.10
Sparse Core Ops, SparseCore 0:
  9.7 49.5 all-gather.18
  121.2 23.0 all-gather.10
  185.8 23.0 all-gather.20
  210.4 24.2 all-gather.22
  267.5 21.1 reduce-scatter.5
  291.7 22.9 reduce-scatter.3
  317.1 23.5 reduce-scatter.7
  342.4 24.2 all-gather.14
  368.5 29.0 all-gather.16
  399.2 43.9 all-gather.12
